TPU v7x, 32 devices: a whole 2x2x4 slice. The times are simulated.
32 devices in a mesh: dp: 2 (over core), row: 4 (over y, x), col: 4 (over z).
Axes of the slice: x: 2, y: 2, z: 4, core: 2. Of those that a mesh axis runs over, the one named last changes fastest.
Arguments:
- inputs: bfloat16 [2048, 1024], P('dp', ('row', 'col')), may hold values from -6 to 6
- first_gain: float32 [1024], P(('row', 'col')), may hold values from 0.25 to 1.75
- first_shift: float32 [1024], P(('row', 'col')), may hold values from -3 to 3
- input_weight: bfloat16 [1024, 3, 1024], P('row', None, 'col'), may hold values from -0.1875 to 0.1875
- input_bias: float32 [2, 1024], P(None, ('col', 'row')), may hold values from -3 to 3
- mixer_weight: bfloat16 [1024, 1024], P('col', 'row'), may hold values from -0.5 to 0.5
- mixer_bias: float32 [1024], P(('row', 'col')), may hold values from -3 to 3
- second_gain: float32 [1024], P(('row', 'col')), may hold values from 0.25 to 1.75
- second_shift: float32 [1024], P(('row', 'col')), may hold values from -3 to 3
- expand_weight: bfloat16 [1024, 4096], P('row', 'col'), may hold values from -0.1875 to 0.1875
- expand_bias: float32 [4096], P(('col', 'row')), may hold values from -3 to 3
- shrink_weight: bfloat16 [4096, 1024], P('col', 'row'), may hold values from -0.09375 to 0.09375
- shrink_bias: float32 [1024], P(('row', 'col')), may hold values from -3 to 3
- cotangent: bfloat16 [2048, 1024], P('dp', ('row', 'col')), may hold values from -6 to 6
Outputs:
- outputs: bfloat16 [2048, 1024], P('dp', ('row', 'col'))
- input_grad: float32 [2048, 1024], P('dp', ('row', 'col'))
- first_gain_grad: float32 [1024], P(('row', 'col'))
- first_shift_grad: float32 [1024], P(('row', 'col'))
- input_weight_grad: float32 [1024, 3, 1024], P('row', None, 'col')
- input_bias_grad: float32 [2, 1024], P(None, ('col', 'row'))
- mixer_weight_grad: float32 [1024, 1024], P('col', 'row')
- mixer_bias_grad: float32 [1024], P(('row', 'col'))
- second_gain_grad: float32 [1024], P(('row', 'col'))
- second_shift_grad: float32 [1024], P(('row', 'col'))
- expand_weight_grad: float32 [1024, 4096], P('row', 'col')
- expand_bias_grad: float32 [4096], P(('col', 'row'))
- shrink_weight_grad: float32 [4096, 1024], P('col', 'row')
- shrink_bias_grad: float32 [1024], P(('row', 'col'))
All inputs are finite; a program needn't handle non-finite values.
Results may differ from a plain program's by a relative error of at most 0.014.
Values may be sent and summed in bfloat16 or wider, within the bound.
A program may use at most 64 MiB of HBM per device.

v0:
```python
import math

import jax
import jax.numpy as jnp
from jax import lax
from jax.sharding import PartitionSpec as P

D = 1024
HD = 64
LEN = 1024


EPSILON = 1e-05
TANH_FACTOR = math.sqrt(2.0 / math.pi)
MASK_FILL = -1e30


def for_sending(array):
    return jax.tree.map(lambda a: a.astype(jnp.bfloat16) if a.dtype == jnp.float32 else a, array)


def gelu_value(preact):
    tanh_input = TANH_FACTOR * (preact + 0.044715 * preact * preact * preact)
    return 0.5 * preact * (1.0 + jnp.tanh(tanh_input))


def gelu_slope(preact):
    tanh_input = TANH_FACTOR * (preact + 0.044715 * preact * preact * preact)
    tangent = jnp.tanh(tanh_input)
    return 0.5 * (1.0 + tangent) + 0.5 * preact * (1.0 - tangent * tangent) * TANH_FACTOR * (
        1.0 + 3.0 * 0.044715 * preact * preact
    )


def norm_forward(values, gain, shift):
    total, squares = lax.psum(
        (jnp.sum(values, axis=1, keepdims=True), jnp.sum(values * values, axis=1, keepdims=True)),
        ("row", "col"),
    )
    center = total / D
    inverse = lax.rsqrt(squares / D - center * center + EPSILON)
    standard = (values - center) * inverse
    return (standard, inverse, (standard * gain + shift).astype(jnp.bfloat16))


def norm_backward(grad_out, standard, inverse, gain):
    scaled = grad_out * gain
    first_sum, second_sum = lax.psum(
        (jnp.sum(scaled, axis=1, keepdims=True), jnp.sum(scaled * standard, axis=1, keepdims=True)),
        ("row", "col"),
    )
    return inverse * (scaled - first_sum / D - standard * (second_sum / D))


def gather_model(activ):
    return lax.all_gather(activ, "col", axis=1, tiled=True)


def gather_units(activ):
    return lax.all_gather(for_sending(activ), "row", axis=1, tiled=True).astype(activ.dtype)


def sum_units(partial_sum):
    return lax.psum_scatter(partial_sum, "row", scatter_dimension=1, tiled=True)


def sum_model(partial_sum):
    return lax.psum_scatter(partial_sum, "col", scatter_dimension=1, tiled=True)


def gather_grad_model(activ):
    return lax.all_gather(activ, "col", axis=1, tiled=True)


def sum_grad_units(partial_sum):
    return lax.psum_scatter(partial_sum, "row", scatter_dimension=1, tiled=True)


def gather_grad_units(activ):
    return lax.all_gather(activ, "row", axis=1, tiled=True)


def sum_grad_model(partial_sum):
    return lax.psum_scatter(partial_sum, "col", scatter_dimension=1, tiled=True)


def block_scores(query_block, key_rows, offset):
    length = key_rows.shape[0]
    block_rows = query_block.shape[0]
    scores = jnp.einsum(
        "qd,kd->qk", query_block, key_rows, preferred_element_type=jnp.float32
    ) * HD ** (-0.5)
    causal = (offset + jnp.arange(block_rows))[:, None] >= jnp.arange(length)[None, :]
    return jnp.where(causal, scores, MASK_FILL)


def attend_forward(packed):
    queries, key_rows, value_rows = packed
    length = queries.shape[0]
    block_rows = min(512, length)
    outputs = []
    totals = []
    for offset in range(0, length, block_rows):
        scores = block_scores(queries[offset : offset + block_rows], key_rows, offset)
        row_max = jnp.max(scores, axis=1, keepdims=True)
        log_total = row_max + jnp.log(jnp.sum(jnp.exp(scores - row_max), axis=1, keepdims=True))
        weights = jnp.exp(scores - log_total).astype(jnp.bfloat16)
        outputs.append(
            jnp.dot(weights, value_rows, preferred_element_type=jnp.float32).astype(jnp.bfloat16)
        )
        totals.append(log_total[:, 0])
    return (jnp.concatenate(outputs, axis=0), jnp.concatenate(totals, axis=0))


def attend_backward(packed):
    queries, key_rows, value_rows, attended, log_total, grad_out = packed
    length = queries.shape[0]
    block_rows = min(512, length)
    score_scale = HD ** (-0.5)
    delta = jnp.sum(
        grad_out.astype(jnp.float32) * attended.astype(jnp.float32), axis=1, keepdims=True
    )
    key_grad = jnp.zeros(key_rows.shape, jnp.float32)
    value_grad = jnp.zeros(value_rows.shape, jnp.float32)
    query_parts = []
    for offset in range(0, length, block_rows):
        query_block = queries[offset : offset + block_rows]
        grad_block = grad_out[offset : offset + block_rows]
        scores = block_scores(query_block, key_rows, offset)
        weights = jnp.exp(scores - log_total[offset : offset + block_rows, None])
        value_grad = value_grad + jnp.einsum(
            "qk,qd->kd",
            weights.astype(jnp.bfloat16),
            grad_block,
            preferred_element_type=jnp.float32,
        )
        grad_weights = jnp.einsum(
            "qd,kd->qk", grad_block, value_rows, preferred_element_type=jnp.float32
        )
        grad_scores = (weights * (grad_weights - delta[offset : offset + block_rows])).astype(
            jnp.bfloat16
        )
        query_parts.append(
            score_scale * jnp.dot(grad_scores, key_rows, preferred_element_type=jnp.float32)
        )
        key_grad = key_grad + score_scale * jnp.einsum(
            "qk,qd->kd", grad_scores, query_block, preferred_element_type=jnp.float32
        )
    return (jnp.concatenate(query_parts, axis=0), key_grad, value_grad)


def shards(
    inputs,
    first_gain,
    first_shift,
    input_weight,
    input_bias,
    mixer_weight,
    mixer_bias,
    second_gain,
    second_shift,
    expand_weight,
    expand_bias,
    shrink_weight,
    shrink_bias,
    cotangent,
):
    tokens = inputs.shape[0]
    sequence_count = tokens // LEN
    values = inputs.astype(jnp.float32)
    first_standard, first_inverse, first_normed = norm_forward(values, first_gain, first_shift)
    first_block = gather_model(first_normed)
    projected = jnp.einsum(
        "td,djn->tjn", first_block, input_weight, preferred_element_type=jnp.float32
    )
    block_width = projected.shape[2]
    projected = sum_units(projected.reshape(tokens * 3, block_width)).reshape(tokens, 3, -1)
    queries = (projected[:, 0] + input_bias[0]).astype(jnp.bfloat16)
    key_rows = projected[:, 1].astype(jnp.bfloat16)
    value_rows = (projected[:, 2] + input_bias[1]).astype(jnp.bfloat16)
    head_width = queries.shape[1]
    query_seqs = queries.reshape(sequence_count, LEN, head_width)
    key_seqs = key_rows.reshape(sequence_count, LEN, head_width)
    value_seqs = value_rows.reshape(sequence_count, LEN, head_width)
    attended_seqs, log_total = lax.map(attend_forward, (query_seqs, key_seqs, value_seqs))
    attended = attended_seqs.reshape(tokens, head_width)
    mixer_block = gather_units(attended)
    attention = (
        sum_model(jnp.dot(mixer_block, mixer_weight, preferred_element_type=jnp.float32))
        + mixer_bias
    )
    middle = values + attention
    second_standard, second_inverse, second_normed = norm_forward(middle, second_gain, second_shift)
    second_block = gather_model(second_normed)
    preact = (
        sum_units(jnp.dot(second_block, expand_weight, preferred_element_type=jnp.float32))
        + expand_bias
    )
    hidden = gelu_value(preact).astype(jnp.bfloat16)
    hidden_block = gather_units(hidden)
    branch = (
        sum_model(jnp.dot(hidden_block, shrink_weight, preferred_element_type=jnp.float32))
        + shrink_bias
    )
    outputs = (middle + branch).astype(jnp.bfloat16)
    upstream = cotangent.astype(jnp.float32)
    shrink_bias_grad = jnp.sum(upstream, axis=0)
    upstream_block = gather_grad_model(cotangent)
    shrink_weight_grad = jnp.einsum(
        "tf,td->fd", hidden_block, upstream_block, preferred_element_type=jnp.float32
    )
    grad_hidden = sum_grad_units(
        jnp.einsum("td,fd->tf", upstream_block, shrink_weight, preferred_element_type=jnp.float32)
    )
    grad_preact = grad_hidden * gelu_slope(preact)
    expand_bias_grad = jnp.sum(grad_preact, axis=0)
    preact_block = gather_grad_units(grad_preact.astype(jnp.bfloat16))
    expand_weight_grad = jnp.einsum(
        "td,tf->df", second_block, preact_block, preferred_element_type=jnp.float32
    )
    grad_second = sum_grad_model(
        jnp.einsum("tf,df->td", preact_block, expand_weight, preferred_element_type=jnp.float32)
    )
    second_gain_grad = jnp.sum(grad_second * second_standard, axis=0)
    second_shift_grad = jnp.sum(grad_second, axis=0)
    grad_middle = upstream + norm_backward(
        grad_second, second_standard, second_inverse, second_gain
    )
    mixer_bias_grad = jnp.sum(grad_middle, axis=0)
    middle_block = gather_grad_model(grad_middle.astype(jnp.bfloat16))
    mixer_weight_grad = jnp.einsum(
        "th,td->hd", mixer_block, middle_block, preferred_element_type=jnp.float32
    )
    grad_attended = sum_grad_units(
        jnp.einsum("td,hd->th", middle_block, mixer_weight, preferred_element_type=jnp.float32)
    ).astype(jnp.bfloat16)
    query_grad, key_grad, value_grad = lax.map(
        attend_backward,
        (
            query_seqs,
            key_seqs,
            value_seqs,
            attended_seqs,
            log_total,
            grad_attended.reshape(sequence_count, LEN, head_width),
        ),
    )
    query_grad = query_grad.reshape(tokens, head_width)
    key_grad = key_grad.reshape(tokens, head_width)
    value_grad = value_grad.reshape(tokens, head_width)
    input_bias_grad = jnp.stack([jnp.sum(query_grad, axis=0), jnp.sum(value_grad, axis=0)])
    stacked = (
        jnp.stack([query_grad, key_grad, value_grad], axis=1)
        .astype(jnp.bfloat16)
        .reshape(tokens * 3, head_width)
    )
    stacked_block = gather_grad_units(stacked).reshape(tokens, 3, -1)
    input_weight_grad = jnp.einsum(
        "td,tjn->djn", first_block, stacked_block, preferred_element_type=jnp.float32
    )
    grad_first = sum_grad_model(
        jnp.einsum("tjn,djn->td", stacked_block, input_weight, preferred_element_type=jnp.float32)
    )
    first_gain_grad = jnp.sum(grad_first * first_standard, axis=0)
    first_shift_grad = jnp.sum(grad_first, axis=0)
    input_grad = grad_middle + norm_backward(grad_first, first_standard, first_inverse, first_gain)
    (
        first_gain_grad,
        first_shift_grad,
        input_weight_grad,
        input_bias_grad,
        mixer_weight_grad,
        mixer_bias_grad,
        second_gain_grad,
        second_shift_grad,
        expand_weight_grad,
        expand_bias_grad,
        shrink_weight_grad,
        shrink_bias_grad,
    ) = lax.psum(
        (
            first_gain_grad,
            first_shift_grad,
            input_weight_grad,
            input_bias_grad,
            mixer_weight_grad,
            mixer_bias_grad,
            second_gain_grad,
            second_shift_grad,
            expand_weight_grad,
            expand_bias_grad,
            shrink_weight_grad,
            shrink_bias_grad,
        ),
        "dp",
    )
    return (
        outputs,
        input_grad,
        first_gain_grad,
        first_shift_grad,
        input_weight_grad,
        input_bias_grad,
        mixer_weight_grad,
        mixer_bias_grad,
        second_gain_grad,
        second_shift_grad,
        expand_weight_grad,
        expand_bias_grad,
        shrink_weight_grad,
        shrink_bias_grad,
    )


def solution(mesh):
    in_specs = (
        P("dp", ("row", "col")),
        P(("row", "col")),
        P(("row", "col")),
        P("row", None, "col"),
        P(None, ("col", "row")),
        P("col", "row"),
        P(("row", "col")),
        P(("row", "col")),
        P(("row", "col")),
        P("row", "col"),
        P(("col", "row")),
        P("col", "row"),
        P(("row", "col")),
        P("dp", ("row", "col")),
    )
    out_specs = (
        P("dp", ("row", "col")),
        P("dp", ("row", "col")),
        P(("row", "col")),
        P(("row", "col")),
        P("row", None, "col"),
        P(None, ("col", "row")),
        P("col", "row"),
        P(("row", "col")),
        P(("row", "col")),
        P(("row", "col")),
        P("row", "col"),
        P(("col", "row")),
        P("col", "row"),
        P(("row", "col")),
    )
    return jax.shard_map(shards, mesh=mesh, in_specs=in_specs, out_specs=out_specs, check_vma=False)
```

profile of v0, /device:TPU:0, one launch (start us, length us, event | category | flops | bytes accessed | tf_op | source)
XLA Modules:
  0.0 622.5 jit_solution(5426340278342916960)
XLA Ops:
  8.3 44.6 %all-reduce.3 = (f32[1024,1]{0,1:T(1,128)S(1)}, f32[1024,1]{0,1:T(1,128)S(1)}) all-reduce(f32[1024,1]{0,1:T(1,128)S(1)} %bitcast.112, f32[1024,1]{0,1:T(1,128)S(1)} %bitcast.111), channel_id=1, replica_groups=mesh['dp'=2,'row'=4,'col'=4] {'row','col'}, use_global_device_ids=true, to_apply=%region_3.0 | all-reduce | flops 2048 | bytes 16384 | tf_op jit(solution)/shard_map/psum | solution.py:36
  53.9 14.8 %all_gather.24 = bf16[1024,256]{0,1:T(8,128)(2,1)S(1)} all-gather(bf16[1024,64]{0,1:T(8,128)(2,1)S(1)} %fusion.23), channel_id=1, replica_groups=mesh['dp'=2,'row'=4,'col'=4] {'col'}, dimensions={1}, use_global_device_ids=true | all-gather | bytes 655360 | tf_op jit(solution)/shard_map/all_gather | solution.py:56
  71.2 4.1 copy.33
  75.2 6.0 reshape.116
  81.2 3.5 copy.40
  85.4 39.9 %reduce-scatter.25.cloned.1.call-done = f32[64,3072]{1,0:T(8,128)} async-done(((f32[256,3072]{1,0:T(8,128)}), f32[64,3072]{1,0:T(8,128)}) %reduce-scatter.25.cloned.1.call-update) | async-done | bytes 786448
  125.3 2.8 copy.41
  128.1 2.5 reshape.117
  138.5 10.2 %all_gather.25 = bf16[1024,256]{0,1:T(8,128)(2,1)S(1)} all-gather(bf16[1024,64]{0,1:T(8,128)(2,1)S(1)} %pad_maximum_fusion.1), channel_id=1, replica_groups=mesh['dp'=2,'row'=4,'col'=4] {'row'}, dimensions={1}, use_global_device_ids=true | all-gather | bytes 655360 | tf_op jit(solution)/shard_map/all_gather | solution.py:60
  150.2 19.6 %all_gather.28 = bf16[1024,256]{0,1:T(8,128)(2,1)S(1)} all-gather(bf16[1024,64]{0,1:T(8,128)(2,1)S(1)} %copy-done.27), channel_id=1, replica_groups=mesh['dp'=2,'row'=4,'col'=4] {'col'}, dimensions={1}, use_global_device_ids=true | all-gather | bytes 655360 | tf_op jit(solution)/shard_map/all_gather | solution.py:72
  169.8 3.9 fusion.66
  173.8 6.7 %reduce-scatter.11.cloned.1.call-done = f32[1024,64]{0,1:T(8,128)} async-done(((f32[1024,256]{0,1:T(8,128)}), f32[1024,64]{0,1:T(8,128)}) %reduce-scatter.11.cloned.1.call-update) | async-done | bytes 262160 | tf_op jit(solution)/shard_map/reduce_scatter | solution.py:68
  181.6 41.8 %all-reduce.2 = (f32[1024,1]{0,1:T(1,128)S(1)}, f32[1024,1]{0,1:T(1,128)S(1)}) all-reduce(f32[1024,1]{0,1:T(1,128)S(1)} %bitcast.107, f32[1024,1]{0,1:T(1,128)S(1)} %bitcast.106), channel_id=1, replica_groups=mesh['dp'=2,'row'=4,'col'=4] {'row','col'}, use_global_device_ids=true, to_apply=%region_13.14 | all-reduce | flops 2048 | bytes 16384 | tf_op jit(solution)/shard_map/psum | solution.py:36
  223.6 14.8 %all_gather.26 = bf16[1024,256]{0,1:T(8,128)(2,1)S(1)} all-gather(bf16[1024,64]{0,1:T(8,128)(2,1)S(1)} %add_convert_fusion.3), channel_id=1, replica_groups=mesh['dp'=2,'row'=4,'col'=4] {'col'}, dimensions={1}, use_global_device_ids=true | all-gather | bytes 655360 | tf_op jit(solution)/shard_map/all_gather | solution.py:56
  238.4 2.7 fusion.64
  241.4 50.8 %reduce-scatter.13.cloned.1.call-done = f32[1024,256]{1,0:T(8,128)} async-done(((f32[1024,1024]{1,0:T(8,128)}), f32[1024,256]{1,0:T(8,128)}) %reduce-scatter.13.cloned.1.call-update) | async-done | bytes 1048592 | tf_op jit(solution)/shard_map/reduce_scatter | solution.py:64
  292.2 3.9 fusion.49
  296.7 34.6 %all-gather.6.cloned.1.call-done = bf16[1024,1024]{1,0:T(8,128)(2,1)} async-done(((bf16[1024,256]{1,0:T(8,128)(2,1)}), bf16[1024,1024]{1,0:T(8,128)(2,1)}) %all-gather.6.cloned.1.call-update) | async-done | bytes 2097168 | tf_op jit(solution)/shard_map/all_gather | solution.py:80
  331.3 3.3 fusion.67
  334.7 33.9 %all-gather.4.cloned.1.call-done = bf16[1024,1024]{1,0:T(8,128)(2,1)} async-done(((bf16[1024,256]{1,0:T(8,128)(2,1)}), bf16[1024,1024]{1,0:T(8,128)(2,1)}) %all-gather.4.cloned.1.call-update) | async-done | bytes 2097168 | tf_op jit(solution)/shard_map/all_gather | solution.py:60
  368.6 3.4 fusion.65
  372.1 26.7 %reduce-scatter.19.cloned.1.call-done = f32[1024,64]{0,1:T(8,128)} async-done(((f32[1024,256]{0,1:T(8,128)}), f32[1024,64]{0,1:T(8,128)}) %reduce-scatter.19.cloned.1.call-update) | async-done | bytes 262160 | tf_op jit(solution)/shard_map/reduce_scatter | solution.py:84
  400.5 41.3 %all-reduce.1 = (f32[1024,1]{0,1:T(1,128)S(1)}, f32[1024,1]{0,1:T(1,128)S(1)}) all-reduce(f32[1024,1]{0,1:T(1,128)S(1)} %bitcast.108, f32[1024,1]{0,1:T(1,128)S(1)} %bitcast.109), channel_id=1, replica_groups=mesh['dp'=2,'row'=4,'col'=4] {'row','col'}, use_global_device_ids=true, to_apply=%region_21.22 | all-reduce | flops 2048 | bytes 16384 | tf_op jit(solution)/shard_map/psum | solution.py:48
  443.0 2.5 fusion.51
  446.3 14.8 %all_gather.30 = bf16[1024,256]{0,1:T(8,128)(2,1)S(1)} all-gather(bf16[1024,64]{0,1:T(8,128)(2,1)S(1)} %convert_element_type.92), channel_id=1, replica_groups=mesh['dp'=2,'row'=4,'col'=4] {'col'}, dimensions={1}, use_global_device_ids=true | all-gather | bytes 655360 | tf_op jit(solution)/shard_map/all_gather | solution.py:72
  463.4 24.6 %reduce-scatter.21.cloned.1.call-done = f32[1024,64]{0,1:T(8,128)} async-done(((f32[1024,256]{0,1:T(8,128)}), f32[1024,64]{0,1:T(8,128)}) %reduce-scatter.21.cloned.1.call-update) | async-done | bytes 262160 | tf_op jit(solution)/shard_map/reduce_scatter | solution.py:76
  497.9 31.0 %all-gather.8.cloned.1.call-done = bf16[3072,256]{0,1:T(8,128)(2,1)} async-done(((bf16[3072,64]{0,1:T(8,128)(2,1)}), bf16[3072,256]{0,1:T(8,128)(2,1)}) %all-gather.8.cloned.1.call-update) | async-done | bytes 1572880 | tf_op jit(solution)/shard_map/all_gather | solution.py:80
  532.8 3.2 convolution_bitcast_fusion
  536.1 3.5 fusion.70
  544.0 19.5 %reduce-scatter.23.cloned.1.call-done = f32[1024,64]{0,1:T(8,128)} async-done(((f32[1024,256]{0,1:T(8,128)}), f32[1024,64]{0,1:T(8,128)}) %reduce-scatter.23.cloned.1.call-update) | async-done | bytes 262160 | tf_op jit(solution)/shard_map/reduce_scatter | solution.py:84
  564.7 3.1 all-reduce.4
  567.8 40.1 %all-reduce = (f32[1024,1]{0,1:T(1,128)S(1)}, f32[1024,1]{0,1:T(1,128)S(1)}) all-reduce(f32[1024,1]{0,1:T(1,128)S(1)} %bitcast.101, f32[1024,1]{0,1:T(1,128)S(1)} %bitcast.102), channel_id=1, replica_groups=mesh['dp'=2,'row'=4,'col'=4] {'row','col'}, use_global_device_ids=true, to_apply=%region_28.29 | all-reduce | flops 2048 | bytes 16384 | tf_op jit(solution)/shard_map/psum | solution.py:48
  (177 shorter events, 49.4 us)
Async XLA Ops:
  7.2 231.2 %copy-start = (bf16[256,1024]{1,0:T(8,128)(2,1)S(1)}, bf16[256,1024]{1,0:T(8,128)(2,1)}, u32[]{:S(2)}) copy-start(bf16[256,1024]{1,0:T(8,128)(2,1)} %param.23) | copy-start | bytes 1572868
  7.2 118.1 %reduce-scatter.25.cloned.1.call-start = ((), (), s32[]{:S(2)}) async-start(), calls=%async_computation.18 | async-start | bytes 3932160
  84.8 95.8 %reduce-scatter.11.cloned.1.call-start = ((), (), s32[]{:S(2)}) async-start(), calls=%async_computation.8 | async-start | bytes 1310720 | tf_op jit(solution)/shard_map/reduce_scatter | solution.py:68
  137.3 11.5 %copy-start.28 = (bf16[256,256]{1,0:T(8,128)(2,1)S(1)}, bf16[256,256]{1,0:T(8,128)(2,1)}, u32[]{:S(2)}) copy-start(bf16[256,256]{1,0:T(8,128)(2,1)} %param.19) | copy-start | bytes 393220
  138.5 11.6 %copy-start.27 = (bf16[1024,64]{0,1:T(8,128)(2,1)S(1)}, bf16[1024,64]{0,1:T(8,128)(2,1)}, u32[]{:S(2)}) copy-start(bf16[1024,64]{0,1:T(8,128)(2,1)} %param.27) | copy-start | bytes 393220
  150.1 91.3 %reduce-scatter.17.cloned.1.call-start = ((), (), s32[]{:S(2)}) async-start(), calls=%async_computation.12 | async-start | bytes 5242880 | tf_op jit(solution)/shard_map/reduce_scatter | solution.py:76
  173.7 6.8 %copy-start.13 = (bf16[1024,64]{0,1:T(8,128)(2,1)S(1)}, bf16[1024,64]{0,1:T(8,128)(2,1)}, u32[]{:S(2)}) copy-start(bf16[1024,64]{0,1:T(8,128)(2,1)} %param.14) | copy-start | bytes 393220
  173.7 6.8 %copy-start.44 = (f32[64]{0:T(128)S(1)}, f32[64]{0:T(128)}, u32[]{:S(2)}) copy-start(f32[64]{0:T(128)} %param.20) | copy-start | bytes 772
  173.7 49.8 %copy-start.34 = (f32[64]{0:T(128)S(1)}, f32[64]{0:T(128)}, u32[]{:S(2)}) copy-start(f32[64]{0:T(128)} %param.21) | copy-start | bytes 772
  173.7 49.8 %copy-start.45 = (f32[64]{0:T(128)S(1)}, f32[64]{0:T(128)}, u32[]{:S(2)}) copy-start(f32[64]{0:T(128)} %param.22) | copy-start | bytes 772
  173.7 118.5 %reduce-scatter.13.cloned.1.call-start = ((), (), s32[]{:S(2)}) async-start(), calls=%async_computation.9 | async-start | bytes 5242880 | tf_op jit(solution)/shard_map/reduce_scatter | solution.py:64
  181.6 41.9 %copy-start.11 = (f32[1024,64]{0,1:T(8,128)}, f32[1024,64]{0,1:T(8,128)S(1)}, u32[]{:S(2)}) copy-start(f32[1024,64]{0,1:T(8,128)S(1)} %get-tuple-element.100) | copy-start | bytes 786436
  241.2 90.1 %all-gather.6.cloned.1.call-start = ((), (), s32[]{:S(2)}) async-start(), calls=%async_computation.13 | async-start | bytes 2621440 | tf_op jit(solution)/shard_map/all_gather | solution.py:80
  296.1 72.5 %all-gather.4.cloned.1.call-start = ((), (), s32[]{:S(2)}) async-start(), calls=%async_computation.10 | async-start | bytes 2621440 | tf_op jit(solution)/shard_map/all_gather | solution.py:60
  296.7 102.1 %reduce-scatter.19.cloned.1.call-start = ((), (), s32[]{:S(2)}) async-start(), calls=%async_computation.14 | async-start | bytes 1310720 | tf_op jit(solution)/shard_map/reduce_scatter | solution.py:84
  334.6 64.2 %copy-start.12 = (f32[1024,64]{0,1:T(8,128)S(1)}, f32[1024,64]{0,1:T(8,128)}, u32[]{:S(2)}) copy-start(f32[1024,64]{0,1:T(8,128)} %copy-done.11) | copy-start | bytes 786436
  334.6 64.2 %copy-start.35 = (f32[64]{0:T(128)S(1)}, f32[64]{0:T(128)}, u32[]{:S(2)}) copy-start(f32[64]{0:T(128)} %param.21) | copy-start | bytes 772
  334.6 108.3 %reduce-scatter.15.cloned.1.call-start = ((), (), s32[]{:S(2)}) async-start(), calls=%async_computation.11 | async-start | bytes 1310720 | tf_op jit(solution)/shard_map/reduce_scatter | solution.py:68
  372.0 116.0 %reduce-scatter.21.cloned.1.call-start = ((), (), s32[]{:S(2)}) async-start(), calls=%async_computation.15 | async-start | bytes 1310720 | tf_op jit(solution)/shard_map/reduce_scatter | solution.py:76
  446.2 43.0 %copy-start.33 = (f32[512]{0:T(512)S(1)}, f32[512]{0:T(512)}, u32[]{:S(2)}) copy-start(f32[512]{0:T(512)} %copy-done.32) | copy-start | bytes 6148
  461.0 30.4 %copy-start.9 = (bf16[1024,256]{0,1:T(8,128)(2,1)}, bf16[1024,256]{0,1:T(8,128)(2,1)S(1)}, u32[]{:S(2)}) copy-start(bf16[1024,256]{0,1:T(8,128)(2,1)S(1)} %all_gather.30) | copy-start | bytes 1572868
  463.4 65.5 %all-gather.8.cloned.1.call-start = ((), (), s32[]{:S(2)}) async-start(), calls=%async_computation.16 | async-start | bytes 1966080 | tf_op jit(solution)/shard_map/all_gather | solution.py:80
  497.9 65.6 %reduce-scatter.23.cloned.1.call-start = ((), (), s32[]{:S(2)}) async-start(), calls=%async_computation.17 | async-start | bytes 1310720 | tf_op jit(solution)/shard_map/reduce_scatter | solution.py:84
  536.1 73.7 %all-reduce.8.cloned.1.call-start = ((), (), s32[]{:S(2)}) async-start(), calls=%async_computation.19 | async-start | bytes 6291456 | tf_op jit(solution)/shard_map/psum | solution.py:280
  543.9 19.6 %copy-start.36 = (f32[64]{0:T(128)S(1)}, f32[64]{0:T(128)}, u32[]{:S(2)}) copy-start(f32[64]{0:T(128)} %param.15) | copy-start | bytes 772
  543.9 20.8 %copy-start.37 = (f32[256]{0:T(256)S(1)}, f32[256]{0:T(256)}, u32[]{:S(2)}) copy-start(f32[256]{0:T(256)} %get-tuple-element.94) | copy-start | bytes 3076
  543.9 20.8 %copy-start.38 = (f32[64]{0:T(128)S(1)}, f32[64]{0:T(128)}, u32[]{:S(2)}) copy-start(f32[64]{0:T(128)} %get-tuple-element.52) | copy-start | bytes 772
  543.9 20.8 %copy-start.39 = (f32[64]{0:T(128)S(1)}, f32[64]{0:T(128)}, u32[]{:S(2)}) copy-start(f32[64]{0:T(128)} %get-tuple-element.68) | copy-start | bytes 772
  543.9 20.8 %copy-start.40 = (f32[64]{0:T(128)S(1)}, f32[64]{0:T(128)}, u32[]{:S(2)}) copy-start(f32[64]{0:T(128)} %get-tuple-element.96) | copy-start | bytes 772
  543.9 20.8 %copy-start.41 = (f32[64]{0:T(128)S(1)}, f32[64]{0:T(128)}, u32[]{:S(2)}) copy-start(f32[64]{0:T(128)} %get-tuple-element.107) | copy-start | bytes 772
  543.9 64.0 %copy-start.15 = (f32[1024,64]{0,1:T(8,128)S(1)}, f32[1024,64]{0,1:T(8,128)}, u32[]{:S(2)}) copy-start(f32[1024,64]{0,1:T(8,128)} %copy-done.14) | copy-start | bytes 786436
  609.7 4.9 copy-start.21
  (26 other events, 49.4 us)
Sparse Core Ops, SparseCore 0:
  84.9 40.3 reduce-scatter.24
  150.2 30.2 reduce-scatter.10
  183.5 53.2 reduce-scatter.16
  241.3 50.8 reduce-scatter.12
  296.2 35.0 all-gather.5
  333.5 35.0 all-gather.3
  371.5 27.2 reduce-scatter.18
  401.7 27.2 reduce-scatter.14
  463.5 24.5 reduce-scatter.20
  498.0 30.8 all-gather.7
  536.2 27.2 reduce-scatter.22
  567.0 22.0 all-reduce.7
where the time goes:
time: 624 us; the launch traced here: 622 us
  waiting for transfers between devices  268 us (43%)
  blocking collectives  245 us (39%)
  matrix products  37.4 us (6%)
  local copies, waits for them, and re-layouts  36.3 us (6%)
  other arithmetic  19.7 us (3%)
  between operations  14.8 us (2%)
    psum x2, blocking collectives, norm_forward(): lax.psum((jnp.sum(values, axis=1, keepdims=True), jnp.sum(values * values...  86.5 us
    psum x2, blocking collectives, norm_backward(): lax.psum((jnp.sum(scaled, axis=1, keepdims=True), jnp.sum(scaled * standa...  81.4 us
    all_gather x2, waiting for transfers between devices, gather_grad_units(): return lax.all_gather(activ, 'row', axis=1, tiled=True)  65.5 us
    reduce_scatter x1, waiting for transfers between devices, sum_units(): return lax.psum_scatter(partial_sum, 'row', scatter_dimension=1, tiled=True)  50.8 us
    reduce_scatter x2, waiting for transfers between devices, sum_grad_model(): return lax.psum_scatter(partial_sum, 'col', scatter_dimension=1, tiled=True)  46.2 us
    unnamed x13, waiting for transfers between devices  40.6 us
    all_gather x2, blocking collectives, gather_grad_model(): return lax.all_gather(activ, 'col', axis=1, tiled=True)  34.4 us
    all_gather x1, waiting for transfers between devices, gather_units(): lax.all_gather(for_sending(activ), 'row', axis=1, tiled=True)  33.9 us
  transfers between devices with their start and end apart: 12, of which 9 were waited for; matrix products, arithmetic and copies ran while one was open for 5% of the time, Pallas kernels for 0%

commit v1 on v0

v1 whole, which is shorter than its diff:
```python
import functools
import math

import jax
import jax.numpy as jnp
from jax import lax
from jax.experimental import pallas as pl
from jax.experimental.pallas import tpu as pltpu
from jax.sharding import PartitionSpec as P

D = 1024
HD = 64
LEN = 1024
EPSILON = 1e-05
TANH_FACTOR = math.sqrt(2.0 / math.pi)
MASK_FILL = -1e30
BF = jnp.bfloat16
F32 = jnp.float32
MESH = pl.DeviceIdType.MESH
VMEM = pl.BlockSpec(memory_space=pltpu.VMEM)


def gelu_both(preact):
    square = preact * preact
    tangent = jnp.tanh(TANH_FACTOR * (preact + 0.044715 * square * preact))
    value = 0.5 * preact * (1.0 + tangent)
    slope = 0.5 * (1.0 + tangent) + 0.5 * preact * (1.0 - tangent * tangent) * TANH_FACTOR * (
        1.0 + 3.0 * 0.044715 * square
    )
    return value, slope


def norm_forward(values, gain, shift):
    center = jnp.mean(values, axis=1, keepdims=True)
    squares = jnp.mean(values * values, axis=1, keepdims=True)
    inverse = lax.rsqrt(squares - center * center + EPSILON)
    standard = (values - center) * inverse
    return (standard, inverse, (standard * gain + shift).astype(BF))


def norm_backward(grad_out, standard, inverse, gain):
    scaled = grad_out * gain
    first = jnp.mean(scaled, axis=1, keepdims=True)
    second = jnp.mean(scaled * standard, axis=1, keepdims=True)
    return inverse * (scaled - first - standard * second)


class Exchange:
    def __init__(self, sizes):
        self.sizes = sizes
        self.calls = 0

    def __call__(self, axes, arrays, gather):
        sizes = [self.sizes[a] for a in axes]
        n = math.prod(sizes)
        count = len(arrays)

        def target(index):
            out = {}
            for axis, size in reversed(list(zip(axes, sizes))):
                out[axis] = lax.rem(index, size)
                index = lax.div(index, size)
            return out

        def kernel(*refs):
            ins, outs = refs[:count], refs[count : 2 * count]
            send_sem, recv_sem = refs[2 * count :]
            me = lax.axis_index(axes[0])
            for axis, size in list(zip(axes, sizes))[1:]:
                me = me * size + lax.axis_index(axis)
            barrier = pltpu.get_barrier_semaphore()
            for k in range(1, n):
                pl.semaphore_signal(
                    barrier, inc=1, device_id=target(lax.rem(me + k, n)), device_id_type=MESH
                )
            pl.semaphore_wait(barrier, n - 1)
            copies = []
            for o in range(count):
                for k in range(1, n):
                    peer = lax.rem(me + k, n)
                    copy = pltpu.make_async_remote_copy(
                        src_ref=ins[o] if gather[o] else ins[o].at[peer],
                        dst_ref=outs[o].at[me],
                        send_sem=send_sem.at[o, k],
                        recv_sem=recv_sem.at[o, k],
                        device_id=target(peer),
                        device_id_type=MESH,
                    )
                    copy.start()
                    copies.append(copy)
            for o in range(count):
                outs[o][me] = ins[o][...] if gather[o] else ins[o][me]
            for copy in copies:
                copy.wait()

        out_shape = [
            jax.ShapeDtypeStruct(((n,) + a.shape) if g else a.shape, a.dtype)
            for a, g in zip(arrays, gather)
        ]
        self.calls += 1
        return pl.pallas_call(
            kernel,
            out_shape=out_shape,
            in_specs=[VMEM] * count,
            out_specs=[VMEM] * count,
            scratch_shapes=[
                pltpu.SemaphoreType.DMA((count, n)),
                pltpu.SemaphoreType.DMA((count, n)),
            ],
            compiler_params=pltpu.CompilerParams(
                collective_id=self.calls, has_side_effects=True
            ),
            name=f"exchange_{self.calls}",
        )(*arrays)


def dot(a, b, dims):
    return lax.dot_general(a, b, (dims, ((), ())), preferred_element_type=F32)


NN = ((1,), (0,))
NT = ((1,), (1,))
TN = ((0,), (0,))


def causal_scores(query, keys, offset):
    scores = dot(query, keys, NT) * HD ** (-0.5)
    rows = offset + lax.broadcasted_iota(jnp.int32, scores.shape, 0)
    columns = lax.broadcasted_iota(jnp.int32, scores.shape, 1)
    return jnp.where(rows >= columns, scores, MASK_FILL)


def attend_forward_kernel(q_ref, k_ref, v_ref, out_ref, total_ref, *, block):
    length = q_ref.shape[0]
    for start in range(0, length, block):
        end = start + block
        scores = causal_scores(q_ref[start:end], k_ref[:end], start)
        row_max = jnp.max(scores, axis=1, keepdims=True)
        powers = jnp.exp(scores - row_max)
        row_sum = jnp.sum(powers, axis=1, keepdims=True)
        weights = (powers * (1.0 / row_sum)).astype(BF)
        out_ref[start:end] = dot(weights, v_ref[:end], NN).astype(BF)
        total_ref[start:end] = row_max + jnp.log(row_sum)


def attend_forward(queries, key_rows, value_rows, block=256):
    length = queries.shape[0]
    return pl.pallas_call(
        functools.partial(attend_forward_kernel, block=block),
        out_shape=[
            jax.ShapeDtypeStruct(queries.shape, BF),
            jax.ShapeDtypeStruct((length, 1), F32),
        ],
        in_specs=[VMEM] * 3,
        out_specs=[VMEM] * 2,
        name="attend_forward",
    )(queries, key_rows, value_rows)


def attend_backward_kernel(
    q_ref, k_ref, v_ref, a_ref, total_ref, g_ref, dq_ref, dk_ref, dv_ref, *, block
):
    length = q_ref.shape[0]
    dk_ref[...] = jnp.zeros_like(dk_ref)
    dv_ref[...] = jnp.zeros_like(dv_ref)
    for start in range(0, length, block):
        end = start + block
        grad = g_ref[start:end]
        query = q_ref[start:end]
        delta = jnp.sum(grad.astype(F32) * a_ref[start:end].astype(F32), axis=1, keepdims=True)
        scores = causal_scores(query, k_ref[:end], start)
        weights = jnp.exp(scores - total_ref[start:end])
        dv_ref[:end] += dot(weights.astype(BF), grad, TN)
        grad_weights = dot(grad, v_ref[:end], NT)
        grad_scores = (weights * (grad_weights - delta)).astype(BF)
        dq_ref[start:end] = HD ** (-0.5) * dot(grad_scores, k_ref[:end], NN)
        dk_ref[:end] += HD ** (-0.5) * dot(grad_scores, query, TN)


def attend_backward(*arrays, block=256):
    shape = jax.ShapeDtypeStruct(arrays[0].shape, F32)
    return pl.pallas_call(
        functools.partial(attend_backward_kernel, block=block),
        out_shape=[shape] * 3,
        in_specs=[VMEM] * 6,
        out_specs=[VMEM] * 3,
        name="attend_backward",
    )(*arrays)


def shards(
    sizes,
    inputs,
    first_gain,
    first_shift,
    input_weight,
    input_bias,
    mixer_weight,
    mixer_bias,
    second_gain,
    second_shift,
    expand_weight,
    expand_bias,
    shrink_weight,
    shrink_bias,
    cotangent,
):
    exchange = Exchange(sizes)
    rows, cols = sizes["row"], sizes["col"]
    n = rows * cols
    tokens, wide = inputs.shape
    part, band = tokens // n, tokens // rows
    width = wide * n
    units = input_weight.shape[2]
    head = units // rows
    both = ("row", "col")

    weight_qkv = lax.all_gather(
        input_weight.reshape(input_weight.shape[0], 3 * units), "row", axis=0, tiled=True
    )
    weight_mix = lax.all_gather(mixer_weight, "row", axis=1, tiled=True)
    weight_up = lax.all_gather(expand_weight, "row", axis=0, tiled=True)
    weight_down = lax.all_gather(shrink_weight, "row", axis=1, tiled=True)

    vectors = jnp.concatenate(
        [
            jnp.stack(
                [first_gain, first_shift, mixer_bias, second_gain, second_shift, shrink_bias]
            ).reshape(-1),
            input_bias.reshape(-1),
            expand_bias,
        ]
    )
    lanes = vectors.shape[0] // 6
    x_parts, cot_parts, vectors = exchange(
        both,
        [
            inputs.reshape(n, part, wide),
            cotangent.reshape(n, part, wide),
            vectors.reshape(6, lanes),
        ],
        [False, False, True],
    )
    vectors = vectors.reshape(n, -1)

    def widen(parts):
        return parts.transpose(1, 0, 2).reshape(part, width)

    values = widen(x_parts).astype(F32)
    cot_part = widen(cot_parts)
    upstream = cot_part.astype(F32)
    full = vectors[:, : 6 * wide].reshape(n, 6, wide).transpose(1, 0, 2).reshape(6, 1, width)
    gain1, shift1, bias_mix, gain2, shift2, bias_down = [full[i] for i in range(6)]
    col = lax.axis_index("col")
    mine = lax.dynamic_index_in_dim(
        vectors[:, 6 * wide :].reshape(rows, cols, -1), col, axis=1, keepdims=False
    )
    bias_in = mine[:, : 2 * head].reshape(rows, 2, head).transpose(1, 0, 2).reshape(2, units)
    bias_up = mine[:, 2 * head :].reshape(1, -1)

    standard1, inverse1, normed1 = norm_forward(values, gain1, shift1)
    normed1_band, cot_band = exchange(("col",), [normed1, cot_part], [True, True])
    normed1_band = normed1_band.reshape(band, width)
    cot_band = cot_band.reshape(band, width)

    projected = dot(normed1_band, weight_qkv, NN)
    bias_qkv = jnp.concatenate([bias_in[0], jnp.zeros_like(bias_in[0]), bias_in[1]])
    qkv = (projected + bias_qkv[None]).astype(BF)
    (qkv_heads,) = exchange(
        ("row",), [qkv.reshape(band, 3, rows, head).transpose(2, 1, 0, 3)], [False]
    )
    qkv_heads = qkv_heads.transpose(1, 0, 2, 3).reshape(3, tokens, head)
    queries, key_rows, value_rows = qkv_heads[0], qkv_heads[1], qkv_heads[2]
    attended_head, log_total = attend_forward(queries, key_rows, value_rows)
    (attended,) = exchange(("row",), [attended_head.reshape(rows, band, head)], [False])
    attended = attended.transpose(1, 0, 2).reshape(band, units)

    def sum_col(partial_sum):
        (pieces,) = exchange(("col",), [partial_sum.astype(BF).reshape(cols, part, width)], [False])
        return jnp.sum(pieces.astype(F32), axis=0)

    def gather_col(piece):
        (pieces,) = exchange(("col",), [piece], [True])
        return pieces.reshape(band, width)

    middle = values + sum_col(dot(attended, weight_mix, NN)) + bias_mix
    standard2, inverse2, normed2 = norm_forward(middle, gain2, shift2)
    normed2_band = gather_col(normed2)
    preact = dot(normed2_band, weight_up, NN) + bias_up
    hidden, slope = gelu_both(preact)
    hidden = hidden.astype(BF)
    grad_preact = dot(cot_band, weight_down, NT) * slope
    preact_low = grad_preact.astype(BF)
    grad_second = sum_col(dot(preact_low, weight_up, NT))
    branch = sum_col(dot(hidden, weight_down, NN))
    outputs = (middle + branch + bias_down).astype(BF)

    grad_middle = upstream + norm_backward(grad_second, standard2, inverse2, gain2)
    middle_band = gather_col(grad_middle.astype(BF))
    (grad_attended,) = exchange(
        ("row",),
        [dot(middle_band, weight_mix, NT).astype(BF).reshape(band, rows, head).transpose(1, 0, 2)],
        [False],
    )
    query_grad, key_grad, value_grad = attend_backward(
        queries,
        key_rows,
        value_rows,
        attended_head,
        log_total,
        grad_attended.reshape(tokens, head),
    )
    input_bias_grad = jnp.stack([jnp.sum(query_grad, axis=0), jnp.sum(value_grad, axis=0)])
    stacked = jnp.stack([query_grad, key_grad, value_grad]).astype(BF)
    (stacked,) = exchange(
        ("row",), [stacked.reshape(3, rows, band, head).transpose(1, 0, 2, 3)], [False]
    )
    stacked = stacked.transpose(2, 1, 0, 3).reshape(band, 3 * units)
    grad_first = sum_col(dot(stacked, weight_qkv, NT))
    input_grad = grad_middle + norm_backward(grad_first, standard1, inverse1, gain1)

    def split_rows(grad):
        return grad.astype(BF)

    def over_row(grad, axis):
        return lax.psum_scatter(
            grad.astype(BF), "row", scatter_dimension=axis, tiled=True
        ).astype(F32)

    shrink_weight_grad = over_row(dot(hidden, cot_band, TN), 1)
    expand_weight_grad = over_row(dot(normed2_band, preact_low, TN), 0)
    mixer_weight_grad = over_row(dot(attended, middle_band, TN), 1)
    input_weight_grad = over_row(dot(normed1_band, stacked, TN), 0).reshape(input_weight.shape)

    shared = jnp.stack(
        [
            jnp.sum(grad_first * standard1, axis=0),
            jnp.sum(grad_first, axis=0),
            jnp.sum(grad_middle, axis=0),
            jnp.sum(grad_second * standard2, axis=0),
            jnp.sum(grad_second, axis=0),
            jnp.sum(upstream, axis=0),
        ]
    )
    up_grad = jnp.sum(grad_preact, axis=0)
    out_parts, in_parts, shared, up_parts = exchange(
        both,
        [
            outputs.reshape(part, n, wide).transpose(1, 0, 2),
            input_grad.astype(BF).reshape(part, n, wide).transpose(1, 0, 2),
            shared.reshape(6, n, wide).transpose(1, 0, 2),
            jnp.broadcast_to(up_grad.reshape(rows, 1, 1, -1), (rows, cols, 1, up_grad.shape[0] // rows)).reshape(n, 1, -1),
        ],
        [False] * 4,
    )
    outputs = out_parts.reshape(tokens, wide)
    input_grad = in_parts.reshape(tokens, wide).astype(F32)
    shared = jnp.sum(shared, axis=0)
    expand_bias_grad = jnp.sum(
        lax.dynamic_index_in_dim(
            up_parts.reshape(rows, cols, -1), col, axis=1, keepdims=False
        ),
        axis=0,
    )
    (
        shared,
        input_weight_grad,
        input_bias_grad,
        mixer_weight_grad,
        expand_weight_grad,
        expand_bias_grad,
        shrink_weight_grad,
    ) = lax.psum(
        (
            shared,
            input_weight_grad,
            input_bias_grad,
            mixer_weight_grad,
            expand_weight_grad,
            expand_bias_grad,
            shrink_weight_grad,
        ),
        "dp",
    )
    return (
        outputs,
        input_grad,
        shared[0],
        shared[1],
        input_weight_grad,
        input_bias_grad,
        mixer_weight_grad,
        shared[2],
        shared[3],
        shared[4],
        expand_weight_grad,
        expand_bias_grad,
        shrink_weight_grad,
        shared[5],
    )


def solution(mesh):
    in_specs = (
        P("dp", ("row", "col")),
        P(("row", "col")),
        P(("row", "col")),
        P("row", None, "col"),
        P(None, ("col", "row")),
        P("col", "row"),
        P(("row", "col")),
        P(("row", "col")),
        P(("row", "col")),
        P("row", "col"),
        P(("col", "row")),
        P("col", "row"),
        P(("row", "col")),
        P("dp", ("row", "col")),
    )
    out_specs = (
        P("dp", ("row", "col")),
        P("dp", ("row", "col")),
        P(("row", "col")),
        P(("row", "col")),
        P("row", None, "col"),
        P(None, ("col", "row")),
        P("col", "row"),
        P(("row", "col")),
        P(("row", "col")),
        P(("row", "col")),
        P("row", "col"),
        P(("col", "row")),
        P("col", "row"),
        P(("row", "col")),
    )
    body = functools.partial(shards, dict(mesh.shape))
    return jax.shard_map(
        body, mesh=mesh, in_specs=in_specs, out_specs=out_specs, check_vma=False
    )
```

time: 624 us -> 409 us (0.66)
  blocking collectives: 245 us -> 30.3 us
  Pallas kernels: 0 us -> 208 us
  waiting for transfers between devices: 268 us -> 79.2 us
  matrix products: 37.4 us -> 27.6 us
  local copies, waits for them, and re-layouts: 36.3 us -> 26.6 us
    pallas_call x0 -> x15, Pallas kernels: none -> 208 us  [the longest x13 199 us: __call__(): pl.pallas_call(kernel, out_shape=out_shape, in_specs=[VMEM] * count, out_...]
    psum x5 -> x1, blocking collectives: 171 us -> 10.5 us  [shards(): lax.psum((shared, input_weight_grad, input_bias_grad, mixer_weight_grad,...]
    all_gather x3, waiting for transfers between devices: 99.5 us -> 0.04 us  [the longest x1 0.02 us: shards(): weight_up = lax.all_gather(expand_weight, 'row', axis=0, tiled=True)]
    all_gather x5 -> x1, blocking collectives: 74.2 us -> 19.8 us  [shards(): weight_mix = lax.all_gather(mixer_weight, 'row', axis=1, tiled=True)]
    reduce_scatter x7 -> x4, waiting for transfers between devices: 128 us -> 77.6 us  [over_row(): lax.psum_scatter(grad.astype(BF), 'row', scatter_dimension=axis, tiled=True)]
    unnamed x13 -> x8, waiting for transfers between devices: 40.6 us -> 1.47 us
    dot_general x24 -> x12, matrix products: 37.4 us -> 27.6 us  [dot(): return lax.dot_general(a, b, (dims, ((), ())), preferred_element_type=F32)]
    reduce_sum x9 -> x14, other arithmetic: 13.6 us -> 9.84 us  [the longest x2 2.29 us: sum_col(): return jnp.sum(pieces.astype(F32), axis=0)]
  transfers between devices with their start and end apart: 12 -> 8, of which waited for: 9 -> 3; matrix products, arithmetic and copies ran while one was open for 5% -> 13% of each run, Pallas kernels for 0% -> 38%
where the time goes in v1:
time: 409 us; the launch traced here: 407 us
  Pallas kernels  208 us (51%)
  waiting for transfers between devices  79.2 us (19%)
  blocking collectives  30.3 us (7%)
  matrix products  27.6 us (7%)
  local copies, waits for them, and re-layouts  26.6 us (7%)
  other arithmetic  20.3 us (5%)
  between operations  14.7 us (4%)
    pallas_call x13, Pallas kernels, __call__(): pl.pallas_call(kernel, out_shape=out_shape, in_specs=[VMEM] * count, out_...  199 us
    reduce_scatter x4, waiting for transfers between devices, over_row(): lax.psum_scatter(grad.astype(BF), 'row', scatter_dimension=axis, tiled=True)  77.6 us
    dot_general x12, matrix products, dot(): return lax.dot_general(a, b, (dims, ((), ())), preferred_element_type=F32)  27.6 us
    all_gather x1, blocking collectives, shards(): weight_mix = lax.all_gather(mixer_weight, 'row', axis=1, tiled=True)  19.8 us
    unnamed x52, local copies, waits for them, and re-layouts  11.8 us
    psum x1, blocking collectives, shards(): lax.psum((shared, input_weight_grad, input_bias_grad, mixer_weight_grad,...  10.5 us
  transfers between devices with their start and end apart: 8, of which 3 were waited for; matrix products, arithmetic and copies ran while one was open for 13% of the time, Pallas kernels for 38%

profile of v1, /device:TPU:0, one launch (start us, length us, event | category | flops | bytes accessed | tf_op | source)
XLA Modules:
  0.0 407.0 jit_solution(15549168172426417482)
XLA Ops:
  7.3 2.0 copy.37
  13.4 22.9 %exchange_1.1 = (bf16[16,64,64]{2,1,0:T(8,128)(2,1)}, bf16[16,64,64]{2,1,0:T(8,128)(2,1)}, f32[16,6,128]{2,1,0:T(8,128)}) custom-call(bf16[16,64,64]{2,1,0:T(8,128)(2,1)} %bitcast.147, bf16[16,64,64]{2,1,0:T(8,128)(2,1)} %bitcast.148, f32[6,128]{1,0:T(8,128)} %maximum_bitcast_fusion.1.refs_2_), custom_call_target="tpu_custom_call" | custom-call | tf_op jit(solution)/shard_map/exchange_1/pallas_call | solution.py:101
  42.8 26.0 %exchange_2.1 = (bf16[4,64,1024]{2,1,0:T(8,128)(2,1)}, bf16[4,64,1024]{2,1,0:T(8,128)(2,1)}) custom-call(bf16[64,1024]{1,0:T(8,128)(2,1)} %add_convert_fusion.3.refs_0_, bf16[64,1024]{1,0:T(8,128)(2,1)} %reshape.450.refs_1_), custom_call_target="tpu_custom_call" | custom-call | tf_op jit(solution)/shard_map/exchange_2/pallas_call | solution.py:101
  68.8 19.8 %all_gather.13 = bf16[256,1024]{1,0:T(8,128)(2,1)S(1)} all-gather(bf16[256,256]{1,0:T(8,128)(2,1)S(1)} %copy-done.8), channel_id=1, replica_groups=mesh['dp'=2,'row'=4,'col'=4] {'row'}, dimensions={1}, use_global_device_ids=true | all-gather | bytes 655360 | tf_op jit(solution)/shard_map/all_gather | solution.py:221
  88.7 2.2 fusion
  92.2 18.1 %exchange_3.1 = bf16[4,3,256,64]{3,2,1,0:T(8,128)(2,1)} custom-call(bf16[4,3,256,64]{3,2,1,0:T(8,128)(2,1)} %bitcast.127), custom_call_target="tpu_custom_call" | custom-call | tf_op jit(solution)/shard_map/exchange_3/pallas_call | solution.py:101
  110.4 2.0 fusion.13
  112.4 4.1 attend_forward.1
  116.5 10.2 %exchange_4.1 = bf16[4,256,64]{2,1,0:T(8,128)(2,1)} custom-call(bf16[4,256,64]{2,1,0:T(8,128)(2,1)} %bitcast.145), custom_call_target="tpu_custom_call" | custom-call | tf_op jit(solution)/shard_map/exchange_4/pallas_call | solution.py:101
  128.9 11.0 %exchange_5.1 = bf16[4,64,1024]{2,1,0:T(8,128)(2,1)} custom-call(bf16[4,64,1024]{2,1,0:T(8,128)(2,1)} %bitcast.137), custom_call_target="tpu_custom_call" | custom-call | tf_op jit(solution)/shard_map/exchange_5/pallas_call | solution.py:101
  142.3 11.7 %exchange_6.1 = bf16[4,64,1024]{2,1,0:T(8,128)(2,1)} custom-call(bf16[64,1024]{1,0:T(8,128)(2,1)} %add_convert_fusion.2.refs_0_), custom_call_target="tpu_custom_call" | custom-call | tf_op jit(solution)/shard_map/exchange_6/pallas_call | solution.py:101
  154.0 3.5 convolution_add_fusion
  157.5 3.2 fusion.17
  162.3 12.0 %exchange_7.1 = bf16[4,64,1024]{2,1,0:T(8,128)(2,1)} custom-call(bf16[4,64,1024]{2,1,0:T(8,128)(2,1)} %bitcast.159), custom_call_target="tpu_custom_call" | custom-call | tf_op jit(solution)/shard_map/exchange_7/pallas_call | solution.py:101
  177.0 14.9 %exchange_9.1 = bf16[4,64,1024]{2,1,0:T(8,128)(2,1)} custom-call(bf16[64,1024]{1,0:T(8,128)(2,1)} %add_convert_fusion.1.refs_0_), custom_call_target="tpu_custom_call" | custom-call | tf_op jit(solution)/shard_map/exchange_9/pallas_call | solution.py:101
  194.2 8.7 %exchange_10.1 = bf16[4,256,64]{2,1,0:T(8,128)(2,1)} custom-call(bf16[4,256,64]{2,1,0:T(8,128)(2,1)} %bitcast.150), custom_call_target="tpu_custom_call" | custom-call | tf_op jit(solution)/shard_map/exchange_10/pallas_call | solution.py:101
  202.9 5.2 %attend_backward.1 = (f32[1024,64]{1,0:T(8,128)}, f32[1024,64]{1,0:T(8,128)}, f32[1024,64]{1,0:T(8,128)}) custom-call(bf16[1024,64]{1,0:T(8,128)(2,1)} %bitcast.134, bf16[1024,64]{1,0:T(8,128)(2,1)} %bitcast.132, bf16[1024,64]{1,0:T(8,128)(2,1)} %bitcast.130, bf16[1024,64]{1,0:T(8,128)(2,1)} %get-tuple-element.32.a_ref, ...), custom_call_target="tpu_custom_call" | custom-call | tf_op jit(solution)/shard_map/attend_backward/pallas_call | solution.py:182
  213.0 10.8 %exchange_11.1 = bf16[4,3,256,64]{3,2,1,0:T(8,128)(2,1)} custom-call(bf16[4,3,256,64]{3,2,1,0:T(8,128)(2,1)} %maximum_bitcast_fusion.refs_0_), custom_call_target="tpu_custom_call" | custom-call | tf_op jit(solution)/shard_map/exchange_11/pallas_call | solution.py:101
  225.3 2.0 convolution_convert_fusion.2
  228.6 29.9 %reduce-scatter.5.cloned.1.call-done = bf16[256,768]{1,0:T(8,128)(2,1)} async-done(((bf16[1024,768]{1,0:T(8,128)(2,1)}), bf16[256,768]{1,0:T(8,128)(2,1)}) %reduce-scatter.5.cloned.1.call-update) | async-done | bytes 393232 | tf_op jit(solution)/shard_map/reduce_scatter | solution.py:326
  258.5 2.0 copy.49
  260.6 3.4 convolution_convert_fusion
  265.1 2.1 convolution_convert_fusion.1
  268.4 3.2 convolution_convert_fusion.6
  271.6 14.6 %exchange_8.1 = bf16[4,64,1024]{2,1,0:T(8,128)(2,1)} custom-call(bf16[4,64,1024]{2,1,0:T(8,128)(2,1)} %bitcast.157), custom_call_target="tpu_custom_call" | custom-call | tf_op jit(solution)/shard_map/exchange_8/pallas_call | solution.py:101
  288.2 2.9 convolution_convert_fusion.7
  291.1 16.7 %exchange_12.1 = bf16[4,64,1024]{2,1,0:T(8,128)(2,1)} custom-call(bf16[4,64,1024]{2,1,0:T(8,128)(2,1)} %bitcast.158), custom_call_target="tpu_custom_call" | custom-call | tf_op jit(solution)/shard_map/exchange_12/pallas_call | solution.py:101
  312.8 21.0 %exchange_13.1 = (bf16[16,64,64]{2,1,0:T(8,128)(2,1)}, bf16[16,64,64]{2,1,0:T(8,128)(2,1)}, f32[16,6,64]{2,1,0:T(8,128)}, f32[16,1,256]{2,1,0:T(1,128)}) custom-call(bf16[16,64,64]{2,1,0:T(8,128)(2,1)} %get-tuple-element.124.refs_0_, bf16[16,64,64]{2,1,0:T(8,128)(2,1)} %fusion.9.refs_1_, f32[16,6,64]{2,1,0:T(8,128)} %bitcast.160, ...), custom_call_target="tpu_custom_call" | custom-call | tf_op jit(solution)/shard_map/exchange_13/pallas_call | solution.py:101
  339.2 2.3 copy.52
  341.5 9.5 %reduce-scatter.11.cloned.1.call-done = bf16[1024,256]{1,0:T(8,128)(2,1)} async-done(((bf16[1024,1024]{1,0:T(8,128)(2,1)}), bf16[1024,256]{1,0:T(8,128)(2,1)}) %reduce-scatter.11.cloned.1.call-update) | async-done | bytes 524304 | tf_op jit(solution)/shard_map/reduce_scatter | solution.py:326
  351.0 38.2 %reduce-scatter.9.cloned.1.call-done = bf16[256,1024]{1,0:T(8,128)(2,1)} async-done(((bf16[1024,1024]{1,0:T(8,128)(2,1)}), bf16[256,1024]{1,0:T(8,128)(2,1)}) %reduce-scatter.9.cloned.1.call-update) | async-done | bytes 524304 | tf_op jit(solution)/shard_map/reduce_scatter | solution.py:326
  389.2 10.5 %all-reduce.5 = (f32[6,64]{1,0:T(8,128)S(1)}, f32[2,64]{1,0:T(2,128)}, f32[256,256]{1,0:T(8,128)}, f32[256,1024]{1,0:T(8,128)}, f32[256]{0:T(256)}, /*index=5*/f32[1024,256]{1,0:T(8,128)}) all-reduce(f32[6,64]{1,0:T(8,128)S(1)} %reduce_sum.238, f32[2,64]{1,0:T(2,128)S(1)} %pad_maximum_fusion.1, ...), channel_id=1, replica_groups=mesh['dp'=2,'row'=4,'col'=4] {'dp'}, use_global_device_ids=true, to_apply=%region_20.21 | all-reduce | flops 590592 | bytes 3545088 | tf_op jit(solution)/shard_map/psum | solution.py:373
  (148 shorter events, 45.5 us)
Async XLA Ops:
  7.2 3.7 copy-start.19
  7.2 3.8 copy-start.15
  7.2 3.8 copy-start.14
  7.2 3.8 copy-start.13
  7.2 3.8 copy-start.12
  7.2 3.8 copy-start.11
  7.2 3.8 copy-start.10
  7.3 3.9 copy-start.6
  7.3 4.7 %copy-start.7 = (bf16[1024,64]{0,1:T(8,128)(2,1)S(1)}, bf16[1024,64]{0,1:T(8,128)(2,1)}, u32[]{:S(2)}) copy-start(bf16[1024,64]{0,1:T(8,128)(2,1)} %param.27) | copy-start | bytes 393220
  7.3 5.6 %copy-start.9 = (f32[256]{0:T(256)S(1)}, f32[256]{0:T(256)}, u32[]{:S(2)}) copy-start(f32[256]{0:T(256)} %param.24) | copy-start | bytes 3076
  7.3 81.4 %all-gather.4.cloned.1.call-start = ((), (), s32[]{:S(2)}) async-start(), calls=%async_computation.4 | async-start | bytes 1966080 | tf_op jit(solution)/shard_map/all_gather | solution.py:218
  9.4 144.7 %all-gather.6.cloned.1.call-start = ((), (), s32[]{:S(2)}) async-start(), calls=%async_computation.5 | async-start | bytes 2621440 | tf_op jit(solution)/shard_map/all_gather | solution.py:222
  10.1 147.4 %all-gather.8.cloned.1.call-start = ((), (), s32[]{:S(2)}) async-start(), calls=%async_computation.6 | async-start | bytes 2621440 | tf_op jit(solution)/shard_map/all_gather | solution.py:223
  10.9 247.6 %reduce-scatter.5.cloned.1.call-start = ((), (), s32[]{:S(2)}) async-start(), calls=%async_computation.7 | async-start | bytes 1966080 | tf_op jit(solution)/shard_map/reduce_scatter | solution.py:326
  36.3 5.3 %copy-start = (bf16[16,64,64]{2,1,0:T(8,128)(2,1)S(1)}, bf16[16,64,64]{2,1,0:T(8,128)(2,1)}, u32[]{:S(2)}) copy-start(bf16[16,64,64]{2,1,0:T(8,128)(2,1)} %get-tuple-element.28) | copy-start | bytes 393220
  39.3 29.5 %copy-start.8 = (bf16[256,256]{1,0:T(8,128)(2,1)S(1)}, bf16[256,256]{1,0:T(8,128)(2,1)}, u32[]{:S(2)}) copy-start(bf16[256,256]{1,0:T(8,128)(2,1)} %param.19) | copy-start | bytes 393220
  154.0 3.5 copy-start.17
  157.5 3.2 copy-start.16
  162.3 13.9 %copy-start.3 = (bf16[64,1024]{1,0:T(8,128)(2,1)S(1)}, bf16[64,1024]{1,0:T(8,128)(2,1)}, u32[]{:S(2)}) copy-start(bf16[64,1024]{1,0:T(8,128)(2,1)} %reshape.450.refs_1_) | copy-start | bytes 393220
  212.0 13.3 %copy-start.5 = (bf16[4,64,1024]{2,1,0:T(8,128)(2,1)S(1)}, bf16[4,64,1024]{2,1,0:T(8,128)(2,1)}, u32[]{:S(2)}) copy-start(bf16[4,64,1024]{2,1,0:T(8,128)(2,1)} %get-tuple-element.31) | copy-start | bytes 1572868
  225.3 2.1 copy-start.1
  227.3 33.3 %copy-start.18 = (bf16[4,64,1024]{2,1,0:T(8,128)(2,1)S(1)}, bf16[4,64,1024]{2,1,0:T(8,128)(2,1)}, u32[]{:S(2)}) copy-start(bf16[4,64,1024]{2,1,0:T(8,128)(2,1)} %get-tuple-element.33) | copy-start | bytes 1572868
  227.3 111.8 %reduce-scatter.7.cloned.1.call-start = ((), (), s32[]{:S(2)}) async-start(), calls=%async_computation.9 | async-start | bytes 655360 | tf_op jit(solution)/shard_map/reduce_scatter | solution.py:326
  228.5 110.7 %all-reduce.4.cloned.1.call-start = ((), (), s32[]{:S(2)}) async-start(), calls=%async_computation.8 | async-start | bytes 1572864 | tf_op jit(solution)/shard_map/psum | solution.py:373
  260.5 90.5 %reduce-scatter.11.cloned.1.call-start = ((), (), s32[]{:S(2)}) async-start(), calls=%async_computation.11 | async-start | bytes 2621440 | tf_op jit(solution)/shard_map/reduce_scatter | solution.py:326
  264.0 1.0 copy-start.2
  264.1 125.1 %reduce-scatter.9.cloned.1.call-start = ((), (), s32[]{:S(2)}) async-start(), calls=%async_computation.10 | async-start | bytes 2621440 | tf_op jit(solution)/shard_map/reduce_scatter | solution.py:326
  267.2 1.3 copy-start.20
  288.2 21.0 %copy-start.4 = (bf16[16,64,64]{2,1,0:T(8,128)(2,1)S(1)}, bf16[16,64,64]{2,1,0:T(8,128)(2,1)}, u32[]{:S(2)}) copy-start(bf16[16,64,64]{2,1,0:T(8,128)(2,1)} %get-tuple-element.30) | copy-start | bytes 393220
Sparse Core Ops, SparseCore 0:
  10.5 35.7 all-gather.3
  48.1 40.2 all-gather.5
  90.3 40.6 all-gather.7
  227.5 30.9 reduce-scatter.4
  261.7 25.0 reduce-scatter.6
  289.6 18.9 all-reduce.3
  311.6 39.3 reduce-scatter.10
  354.0 35.1 reduce-scatter.8

commit v2 on v1

v2 whole, which is shorter than its diff:
```python
import functools
import math

import jax
import jax.numpy as jnp
from jax import lax
from jax.experimental import pallas as pl
from jax.experimental.pallas import tpu as pltpu
from jax.sharding import PartitionSpec as P

D = 1024
HD = 64
LEN = 1024
EPSILON = 1e-05
TANH_FACTOR = math.sqrt(2.0 / math.pi)
MASK_FILL = -1e30
BF = jnp.bfloat16
F32 = jnp.float32
MESH = pl.DeviceIdType.MESH
VMEM = pl.BlockSpec(memory_space=pltpu.VMEM)


def gelu_both(preact):
    square = preact * preact
    tangent = jnp.tanh(TANH_FACTOR * (preact + 0.044715 * square * preact))
    value = 0.5 * preact * (1.0 + tangent)
    slope = 0.5 * (1.0 + tangent) + 0.5 * preact * (1.0 - tangent * tangent) * TANH_FACTOR * (
        1.0 + 3.0 * 0.044715 * square
    )
    return value, slope


def norm_forward(values, gain, shift):
    center = jnp.mean(values, axis=1, keepdims=True)
    squares = jnp.mean(values * values, axis=1, keepdims=True)
    inverse = lax.rsqrt(squares - center * center + EPSILON)
    standard = (values - center) * inverse
    return (standard, inverse, (standard * gain + shift).astype(BF))


def norm_backward(grad_out, standard, inverse, gain):
    scaled = grad_out * gain
    first = jnp.mean(scaled, axis=1, keepdims=True)
    second = jnp.mean(scaled * standard, axis=1, keepdims=True)
    return inverse * (scaled - first - standard * second)


def whole(ref, index):
    return ref


def lead(ref, index):
    return ref.at[index]


def second(ref, index):
    return ref.at[:, index]


def lanes_of(size):
    return lambda ref, index: ref.at[:, pl.ds(pl.multiple_of(index * size, size), size)]


class Exchange:
    def __init__(self, sizes):
        self.sizes = dict(sizes, pair=2)
        self.calls = 0

    def __call__(self, *items):
        count = len(items)
        groups = []
        for axes in sorted({item[0] for item in items}, key=len, reverse=True):
            if not any(set(axes) < set(other) for other in groups):
                groups.append(axes)
        most = max(math.prod(self.sizes[a] for a in item[0]) for item in items)

        def size_of(axes):
            return math.prod(self.sizes[a] for a in axes)

        def position(axes):
            me = 0
            for axis in axes:
                if axis == "pair":
                    me = lax.rem(lax.axis_index("dp"), 2)
                else:
                    me = me * self.sizes[axis] + lax.axis_index(axis)
            return me

        def target(axes, index):
            out = {}
            for axis in reversed(axes):
                if axis == "pair":
                    dp = lax.axis_index("dp")
                    out["dp"] = dp - lax.rem(dp, 2) + index
                else:
                    out[axis] = lax.rem(index, self.sizes[axis])
                    index = lax.div(index, self.sizes[axis])
            return out

        def kernel(*refs):
            ins, outs = refs[:count], refs[count : 2 * count]
            send_sem, recv_sem, own_sem = refs[2 * count :]
            barrier = pltpu.get_barrier_semaphore()
            greeted = 0
            for axes in groups:
                n, me = size_of(axes), position(axes)
                for k in range(1, n):
                    pl.semaphore_signal(
                        barrier,
                        inc=1,
                        device_id=target(axes, lax.rem(me + k, n)),
                        device_id_type=MESH,
                    )
                greeted += n - 1
            pl.semaphore_wait(barrier, greeted)
            copies = []
            for o, (axes, _, _, src, dst) in enumerate(items):
                n, me = size_of(axes), position(axes)
                for k in range(1, n):
                    peer = lax.rem(me + k, n)
                    copies.append(
                        pltpu.make_async_remote_copy(
                            src_ref=src(ins[o], peer),
                            dst_ref=dst(outs[o], me),
                            send_sem=send_sem.at[o, k],
                            recv_sem=recv_sem.at[o, k],
                            device_id=target(axes, peer),
                            device_id_type=MESH,
                        )
                    )
                    copies[-1].start()
            for o, (axes, _, _, src, dst) in enumerate(items):
                me = position(axes)
                copies.append(
                    pltpu.make_async_copy(src(ins[o], me), dst(outs[o], me), own_sem.at[o])
                )
                copies[-1].start()
            for copy in copies:
                copy.wait()

        self.calls += 1
        return pl.pallas_call(
            kernel,
            out_shape=[jax.ShapeDtypeStruct(i[2], i[1].dtype) for i in items],
            in_specs=[VMEM] * count,
            out_specs=[VMEM] * count,
            scratch_shapes=[
                pltpu.SemaphoreType.DMA((count, most)),
                pltpu.SemaphoreType.DMA((count, most)),
                pltpu.SemaphoreType.DMA((count,)),
            ],
            compiler_params=pltpu.CompilerParams(
                collective_id=self.calls, has_side_effects=True
            ),
            name=f"exchange_{self.calls}",
        )(*[i[1] for i in items])


def dot(a, b, dims):
    return lax.dot_general(a, b, (dims, ((), ())), preferred_element_type=F32)


NN = ((1,), (0,))
NT = ((1,), (1,))
TN = ((0,), (0,))


def causal_scores(query, keys, offset):
    scores = dot(query, keys, NT) * HD ** (-0.5)
    rows = offset + lax.broadcasted_iota(jnp.int32, scores.shape, 0)
    columns = lax.broadcasted_iota(jnp.int32, scores.shape, 1)
    return jnp.where(rows >= columns, scores, MASK_FILL)


def attend_forward_kernel(q_ref, k_ref, v_ref, out_ref, total_ref, *, block):
    length = q_ref.shape[0]
    for start in range(0, length, block):
        end = start + block
        scores = causal_scores(q_ref[start:end], k_ref[:end], start)
        row_max = jnp.max(scores, axis=1, keepdims=True)
        powers = jnp.exp(scores - row_max)
        row_sum = jnp.sum(powers, axis=1, keepdims=True)
        weights = (powers * (1.0 / row_sum)).astype(BF)
        out_ref[start:end] = dot(weights, v_ref[:end], NN).astype(BF)
        total_ref[start:end] = row_max + jnp.log(row_sum)


def attend_forward(queries, key_rows, value_rows, block=256):
    length = queries.shape[0]
    return pl.pallas_call(
        functools.partial(attend_forward_kernel, block=block),
        out_shape=[
            jax.ShapeDtypeStruct(queries.shape, BF),
            jax.ShapeDtypeStruct((length, 1), F32),
        ],
        in_specs=[VMEM] * 3,
        out_specs=[VMEM] * 2,
        name="attend_forward",
    )(queries, key_rows, value_rows)


def attend_backward_kernel(
    q_ref, k_ref, v_ref, a_ref, total_ref, g_ref, dq_ref, dk_ref, dv_ref, *, block
):
    length = q_ref.shape[0]
    dk_ref[...] = jnp.zeros_like(dk_ref)
    dv_ref[...] = jnp.zeros_like(dv_ref)
    for start in range(0, length, block):
        end = start + block
        grad = g_ref[start:end]
        query = q_ref[start:end]
        delta = jnp.sum(grad.astype(F32) * a_ref[start:end].astype(F32), axis=1, keepdims=True)
        scores = causal_scores(query, k_ref[:end], start)
        weights = jnp.exp(scores - total_ref[start:end])
        dv_ref[:end] += dot(weights.astype(BF), grad, TN)
        grad_weights = dot(grad, v_ref[:end], NT)
        grad_scores = (weights * (grad_weights - delta)).astype(BF)
        dq_ref[start:end] = HD ** (-0.5) * dot(grad_scores, k_ref[:end], NN)
        dk_ref[:end] += HD ** (-0.5) * dot(grad_scores, query, TN)


def attend_backward(*arrays, block=256):
    shape = jax.ShapeDtypeStruct(arrays[0].shape, F32)
    return pl.pallas_call(
        functools.partial(attend_backward_kernel, block=block),
        out_shape=[shape] * 3,
        in_specs=[VMEM] * 6,
        out_specs=[VMEM] * 3,
        name="attend_backward",
    )(*arrays)


def shards(
    sizes,
    inputs,
    first_gain,
    first_shift,
    input_weight,
    input_bias,
    mixer_weight,
    mixer_bias,
    second_gain,
    second_shift,
    expand_weight,
    expand_bias,
    shrink_weight,
    shrink_bias,
    cotangent,
):
    exchange = Exchange(sizes)
    rows, cols = sizes["row"], sizes["col"]
    n = rows * cols
    tokens, wide = inputs.shape
    part, band = tokens // n, tokens // rows
    width = wide * n
    deep, units = input_weight.shape[0], input_weight.shape[2]
    ff = expand_weight.shape[1]
    head = units // rows
    both, row, col, pair = ("row", "col"), ("row",), ("col",), ("pair",)
    pair_me = lax.rem(lax.axis_index("dp"), 2)

    def swap(axes, array):
        return (axes, array, array.shape, lead, lead)

    def gather(axes, array):
        size = math.prod(exchange.sizes[a] for a in axes)
        return (axes, array, (size,) + array.shape, whole, lead)

    def my_half(ref, index):
        return ref.at[lax.rem(lax.axis_index("dp"), 2)]

    def rows_start(weight):
        d, w = weight.shape
        return (row, weight.reshape(2, d // 2, w), (rows, d // 2, w), my_half, lead)

    def rows_finish(half):
        _, d, w = half.shape
        return (pair, half, (rows, 2, d, w), whole, second)

    def lanes_start(weight):
        d, w = weight.shape
        return (row, weight.reshape(2, d // 2, w), (d // 2, rows * w), my_half, lanes_of(w))

    def lanes_finish(half):
        return gather(pair, half)

    def grad_rows_pair(grad):
        d, w = grad.shape
        return (pair, grad.astype(BF), (2, d, w // 2), lanes_of(w // 2), lead)

    def grad_rows_send(pieces):
        half = jnp.sum(pieces.astype(F32), axis=0).astype(BF)
        d, w = half.shape
        return swap(row, half.reshape(rows, d // rows, w))

    def grad_rows_finish(pieces):
        half = jnp.sum(pieces.astype(F32), axis=0)
        d, w = half.shape
        return (pair, half, (d, 2 * w), whole, lanes_of(w))

    def grad_lanes_pair(grad):
        d, w = grad.shape
        return swap(pair, grad.astype(BF).reshape(2, d // 2, w))

    def grad_lanes_send(pieces):
        half = jnp.sum(pieces.astype(F32), axis=0).astype(BF)
        d, w = half.shape
        return (row, half, (rows, d, w // rows), lanes_of(w // rows), lead)

    def grad_lanes_finish(pieces):
        return gather(pair, jnp.sum(pieces.astype(F32), axis=0))

    def scatter_col(partial_sum):
        return swap(col, partial_sum.astype(BF).reshape(cols, -1, width))

    def total(pieces):
        return jnp.sum(pieces.astype(F32), axis=0)

    vectors = jnp.concatenate(
        [
            jnp.stack(
                [first_gain, first_shift, mixer_bias, second_gain, second_shift, shrink_bias]
            ).reshape(-1),
            input_bias.reshape(-1),
            expand_bias,
        ]
    )
    x_parts, cot_parts, vectors, qkv_half = exchange(
        swap(both, inputs.reshape(n, part, wide)),
        swap(both, cotangent.reshape(n, part, wide)),
        gather(both, vectors.reshape(6, -1)),
        rows_start(input_weight.reshape(deep, 3 * units)),
    )
    vectors = vectors.reshape(n, -1)

    def widen(parts):
        return parts.transpose(1, 0, 2).reshape(part, width)

    values = widen(x_parts).astype(F32)
    cot_part = widen(cot_parts)
    upstream = cot_part.astype(F32)
    full = vectors[:, : 6 * wide].reshape(n, 6, wide).transpose(1, 0, 2).reshape(6, 1, width)
    gain1, shift1, bias_mix, gain2, shift2, bias_down = [full[i] for i in range(6)]
    col_me = lax.axis_index("col")
    mine = lax.dynamic_index_in_dim(
        vectors[:, 6 * wide :].reshape(rows, cols, -1), col_me, axis=1, keepdims=False
    )
    bias_in = mine[:, : 2 * head].reshape(rows, 2, head).transpose(1, 0, 2).reshape(2, units)
    bias_up = mine[:, 2 * head :].reshape(1, -1)

    standard1, inverse1, normed1 = norm_forward(values, gain1, shift1)
    normed1_band, weight_qkv, mix_half, up_half = exchange(
        gather(col, normed1),
        rows_finish(qkv_half),
        lanes_start(mixer_weight),
        rows_start(expand_weight),
    )
    normed1_band = normed1_band.reshape(band, width)
    weight_qkv = weight_qkv.reshape(width, 3 * units)

    projected = dot(normed1_band, weight_qkv, NN)
    bias_qkv = jnp.concatenate([bias_in[0], jnp.zeros_like(bias_in[0]), bias_in[1]])
    qkv = (projected + bias_qkv[None]).astype(BF)
    qkv_heads, weight_mix, weight_up, cot_first = exchange(
        swap(row, qkv.reshape(band, 3, rows, head).transpose(2, 1, 0, 3)),
        lanes_finish(mix_half),
        rows_finish(up_half),
        gather(col, cot_part[: part // 2]),
    )
    weight_mix = weight_mix.reshape(units, width)
    weight_up = weight_up.reshape(width, ff)
    qkv_heads = qkv_heads.transpose(1, 0, 2, 3).reshape(3, tokens, head)
    queries, key_rows, value_rows = qkv_heads[0], qkv_heads[1], qkv_heads[2]
    attended_head, log_total = attend_forward(queries, key_rows, value_rows)
    attended, cot_second = exchange(
        swap(row, attended_head.reshape(rows, band, head)),
        gather(col, cot_part[part // 2 :]),
    )
    attended = attended.transpose(1, 0, 2).reshape(band, units)
    cot_band = jnp.concatenate([cot_first, cot_second], axis=1).reshape(band, width)

    attention, down_half = exchange(
        scatter_col(dot(attended, weight_mix, NN)), lanes_start(shrink_weight)
    )
    middle = values + total(attention) + bias_mix
    standard2, inverse2, normed2 = norm_forward(middle, gain2, shift2)
    normed2_band, weight_down = exchange(gather(col, normed2), lanes_finish(down_half))
    normed2_band = normed2_band.reshape(band, width)
    weight_down = weight_down.reshape(ff, width)
    preact = dot(normed2_band, weight_up, NN) + bias_up
    hidden, slope = gelu_both(preact)
    hidden = hidden.astype(BF)
    grad_preact = dot(cot_band, weight_down, NT) * slope
    preact_low = grad_preact.astype(BF)
    grad_second, down_pair, up_pair = exchange(
        scatter_col(dot(preact_low, weight_up, NT)),
        grad_lanes_pair(dot(hidden, cot_band, TN)),
        grad_rows_pair(dot(normed2_band, preact_low, TN)),
    )
    grad_second = total(grad_second)
    grad_middle = upstream + norm_backward(grad_second, standard2, inverse2, gain2)
    middle_band, down_pieces = exchange(
        gather(col, grad_middle.astype(BF)), grad_lanes_send(down_pair)
    )
    middle_band = middle_band.reshape(band, width)
    branch = dot(hidden, weight_down, NN).astype(BF).reshape(cols, part, width)
    grad_attended, branch_first, mix_pair = exchange(
        swap(
            row,
            dot(middle_band, weight_mix, NT)
            .astype(BF)
            .reshape(band, rows, head)
            .transpose(1, 0, 2),
        ),
        swap(col, branch[:, : part // 2]),
        grad_lanes_pair(dot(attended, middle_band, TN)),
    )
    query_grad, key_grad, value_grad = attend_backward(
        queries,
        key_rows,
        value_rows,
        attended_head,
        log_total,
        grad_attended.reshape(tokens, head),
    )
    input_bias_grad = jnp.stack([jnp.sum(query_grad, axis=0), jnp.sum(value_grad, axis=0)])
    stacked = jnp.stack([query_grad, key_grad, value_grad]).astype(BF)
    stacked, branch_second, mix_pieces = exchange(
        swap(row, stacked.reshape(3, rows, band, head).transpose(1, 0, 2, 3)),
        swap(col, branch[:, part // 2 :]),
        grad_lanes_send(mix_pair),
    )
    stacked = stacked.transpose(2, 1, 0, 3).reshape(band, 3 * units)
    branch = jnp.concatenate([total(branch_first), total(branch_second)], axis=0)
    outputs = (middle + branch + bias_down).astype(BF)
    grad_first, up_pieces, in_pair = exchange(
        scatter_col(dot(stacked, weight_qkv, NT)),
        grad_rows_send(up_pair),
        grad_rows_pair(dot(normed1_band, stacked, TN)),
    )
    grad_first = total(grad_first)
    input_grad = grad_middle + norm_backward(grad_first, standard1, inverse1, gain1)

    shared = jnp.stack(
        [
            jnp.sum(grad_first * standard1, axis=0),
            jnp.sum(grad_first, axis=0),
            jnp.sum(grad_middle, axis=0),
            jnp.sum(grad_second * standard2, axis=0),
            jnp.sum(grad_second, axis=0),
            jnp.sum(upstream, axis=0),
        ]
    )
    up_bias = jnp.sum(grad_preact, axis=0).reshape(rows, 1, -1)
    (
        out_parts,
        in_parts,
        shared,
        up_bias,
        in_pieces,
        down_grad,
        up_grad,
        mix_grad,
    ) = exchange(
        swap(both, outputs.reshape(part, n, wide).transpose(1, 0, 2)),
        swap(both, input_grad.astype(BF).reshape(part, n, wide).transpose(1, 0, 2)),
        swap(both, shared.reshape(6, n, wide).transpose(1, 0, 2)),
        swap(row, up_bias),
        grad_rows_send(in_pair),
        grad_lanes_finish(down_pieces),
        grad_rows_finish(up_pieces),
        grad_lanes_finish(mix_pieces),
    )
    outputs = out_parts.reshape(tokens, wide)
    input_grad = in_parts.reshape(tokens, wide).astype(F32)
    small = jnp.concatenate(
        [
            jnp.sum(shared, axis=0).reshape(-1),
            input_bias_grad.reshape(-1),
            jnp.sum(up_bias, axis=0).reshape(-1),
        ]
    )
    in_grad, small = exchange(grad_rows_finish(in_pieces), gather(pair, small.reshape(6, -1)))
    small = jnp.sum(small, axis=0).reshape(-1)
    grads = (small, in_grad, mix_grad, up_grad, down_grad)
    if sizes["dp"] > 2:
        groups = [list(range(i, sizes["dp"], 2)) for i in range(2)]
        grads = lax.psum(grads, "dp", axis_index_groups=groups)
    small, in_grad, mix_grad, up_grad, down_grad = grads
    shared = small[: 6 * wide].reshape(6, wide)
    return (
        outputs,
        input_grad,
        shared[0],
        shared[1],
        in_grad.reshape(input_weight.shape),
        small[6 * wide : 6 * wide + 2 * head].reshape(2, head),
        mix_grad.reshape(mixer_weight.shape),
        shared[2],
        shared[3],
        shared[4],
        up_grad,
        small[6 * wide + 2 * head :],
        down_grad.reshape(shrink_weight.shape),
        shared[5],
    )


def solution(mesh):
    in_specs = (
        P("dp", ("row", "col")),
        P(("row", "col")),
        P(("row", "col")),
        P("row", None, "col"),
        P(None, ("col", "row")),
        P("col", "row"),
        P(("row", "col")),
        P(("row", "col")),
        P(("row", "col")),
        P("row", "col"),
        P(("col", "row")),
        P("col", "row"),
        P(("row", "col")),
        P("dp", ("row", "col")),
    )
    out_specs = (
        P("dp", ("row", "col")),
        P("dp", ("row", "col")),
        P(("row", "col")),
        P(("row", "col")),
        P("row", None, "col"),
        P(None, ("col", "row")),
        P("col", "row"),
        P(("row", "col")),
        P(("row", "col")),
        P(("row", "col")),
        P("row", "col"),
        P(("col", "row")),
        P("col", "row"),
        P(("row", "col")),
    )
    body = functools.partial(shards, dict(mesh.shape))
    return jax.shard_map(
        body, mesh=mesh, in_specs=in_specs, out_specs=out_specs, check_vma=False
    )
```

time: 409 us -> 320 us (0.78)
  waiting for transfers between devices: 79.2 us -> 0 us
  blocking collectives: 30.3 us -> 0 us
  other arithmetic: 20.3 us -> 40.7 us
  Pallas kernels: 208 us -> 222 us
  between operations: 14.7 us -> 1.33 us
  local copies, waits for them, and re-layouts: 26.6 us -> 32.4 us
  matrix products: 27.6 us -> 22.6 us
    reduce_scatter x4 -> x0, waiting for transfers between devices: 77.6 us -> none  [over_row(): lax.psum_scatter(grad.astype(BF), 'row', scatter_dimension=axis, tiled=True)]
    all_gather x1 -> x0, blocking collectives: 19.8 us -> none  [shards(): weight_mix = lax.all_gather(mixer_weight, 'row', axis=1, tiled=True)]
    reduce_sum x4 -> x15, other arithmetic: 3.17 us -> 22.6 us  [the longest x2 4.61 us: grad_rows_send(): half = jnp.sum(pieces.astype(F32), axis=0).astype(BF)]
    pallas_call x13, Pallas kernels: 199 us -> 212 us  [__call__(): pl.pallas_call(kernel, out_shape=[jax.ShapeDtypeStruct(i[2], i[1].dtype)...]
    psum x1 -> x0, blocking collectives: 10.5 us -> none  [shards(): lax.psum((shared, input_weight_grad, input_bias_grad, mixer_weight_grad,...]
    dot_general x12, matrix products: 27.6 us -> 22.6 us  [dot(): return lax.dot_general(a, b, (dims, ((), ())), preferred_element_type=F32)]
    unnamed x52 -> x84, local copies, waits for them, and re-layouts: 11.8 us -> 11.2 us
  transfers between devices with their start and end apart: 8 -> 0, of which waited for: 3 -> 0; matrix products, arithmetic and copies ran while one was open for 13% -> 0% of each run, Pallas kernels for 38% -> 0%
where the time goes in v2:
time: 320 us; the launch traced here: 319 us
  Pallas kernels  222 us (69%)
  other arithmetic  40.7 us (13%)
  local copies, waits for them, and re-layouts  32.4 us (10%)
  matrix products  22.6 us (7%)
    pallas_call x13, Pallas kernels, __call__(): pl.pallas_call(kernel, out_shape=[jax.ShapeDtypeStruct(i[2], i[1].dtype)...  212 us
    dot_general x12, matrix products, dot(): return lax.dot_general(a, b, (dims, ((), ())), preferred_element_type=F32)  22.6 us
    unnamed x84, local copies, waits for them, and re-layouts  11.2 us

profile of v2, /device:TPU:0, one launch (start us, length us, event | category | flops | bytes accessed | tf_op | source)
XLA Modules:
  0.0 318.6 jit_solution(2869927641405680427)
XLA Ops:
  9.5 26.0 %exchange_1.1 = (bf16[16,64,64]{2,1,0:T(8,128)(2,1)}, bf16[16,64,64]{2,1,0:T(8,128)(2,1)}, f32[16,6,128]{2,1,0:T(8,128)}, bf16[4,128,768]{2,1,0:T(8,128)(2,1)}) custom-call(bf16[16,64,64]{2,1,0:T(8,128)(2,1)} %bitcast.168, bf16[16,64,64]{2,1,0:T(8,128)(2,1)} %bitcast.169, f32[6,128]{1,0:T(8,128)} %maximum_bitcast_fusion.1.refs_2_, ...), custom_call_target="tpu_custom_call" | custom-call | tf_op jit(solution)/shard_map/exchange_1/pallas_call | solution.py:142
  44.7 21.0 %exchange_2.1 = (bf16[4,64,1024]{2,1,0:T(8,128)(2,1)}, bf16[4,2,128,768]{3,2,1,0:T(8,128)(2,1)}, bf16[128,1024]{1,0:T(8,128)(2,1)}, bf16[4,128,1024]{2,1,0:T(8,128)(2,1)}) custom-call(bf16[64,1024]{1,0:T(8,128)(2,1)} %add_convert_fusion.3.refs_0_, bf16[4,128,768]{2,1,0:T(8,128)(2,1)} %get-tuple-element.63.refs_1_, bf16[2,128,256]{2,1,0:T(8,128)(2,1)} %bitcast.195, ...), custom_call_target="tpu_custom_call" | custom-call | tf_op jit(solution)/shard_map/exchange_2/pallas_call | solution.py:142
  65.8 2.1 fusion
  69.3 15.8 %exchange_3.1 = (bf16[4,3,256,64]{3,2,1,0:T(8,128)(2,1)}, bf16[2,128,1024]{2,1,0:T(8,128)(2,1)}, bf16[4,2,128,1024]{3,2,1,0:T(8,128)(2,1)}, bf16[4,32,1024]{2,1,0:T(8,128)(2,1)}) custom-call(bf16[4,3,256,64]{3,2,1,0:T(8,128)(2,1)} %bitcast.145, bf16[128,1024]{1,0:T(8,128)(2,1)} %get-tuple-element.66.refs_1_, ...), custom_call_target="tpu_custom_call" | custom-call | tf_op jit(solution)/shard_map/exchange_3/pallas_call | solution.py:142
  85.1 2.1 fusion.13
  87.1 4.1 %attend_forward.1 = (bf16[1024,64]{1,0:T(8,128)(2,1)}, f32[1024,1]{1,0:T(8,128)}) custom-call(bf16[1024,64]{1,0:T(8,128)(2,1)} %bitcast.151, bf16[1024,64]{1,0:T(8,128)(2,1)} %bitcast.149, bf16[1024,64]{1,0:T(8,128)(2,1)} %bitcast.147), custom_call_target="tpu_custom_call" | custom-call | tf_op jit(solution)/shard_map/attend_forward/pallas_call | solution.py:190
  91.2 9.4 %exchange_4.1 = (bf16[4,256,64]{2,1,0:T(8,128)(2,1)}, bf16[4,32,1024]{2,1,0:T(8,128)(2,1)}) custom-call(bf16[4,256,64]{2,1,0:T(8,128)(2,1)} %bitcast.167, bf16[32,1024]{1,0:T(8,128)(2,1)} %slice.119.refs_1_), custom_call_target="tpu_custom_call" | custom-call | tf_op jit(solution)/shard_map/exchange_4/pallas_call | solution.py:142
  101.7 1.8 pad_maximum_fusion
  104.6 15.6 %exchange_5.1 = (bf16[4,64,1024]{2,1,0:T(8,128)(2,1)}, bf16[512,1024]{1,0:T(8,128)(2,1)}) custom-call(bf16[4,64,1024]{2,1,0:T(8,128)(2,1)} %bitcast.161, bf16[2,512,256]{2,1,0:T(8,128)(2,1)} %bitcast.182), custom_call_target="tpu_custom_call" | custom-call | tf_op jit(solution)/shard_map/exchange_5/pallas_call | solution.py:142
  122.6 15.8 %exchange_6.1 = (bf16[4,64,1024]{2,1,0:T(8,128)(2,1)}, bf16[2,512,1024]{2,1,0:T(8,128)(2,1)}) custom-call(bf16[64,1024]{1,0:T(8,128)(2,1)} %add_convert_fusion.2.refs_0_, bf16[512,1024]{1,0:T(8,128)(2,1)} %get-tuple-element.76.refs_1_), custom_call_target="tpu_custom_call" | custom-call | tf_op jit(solution)/shard_map/exchange_6/pallas_call | solution.py:142
  138.4 2.6 convolution_add_fusion
  142.0 1.8 fusion.19
  146.3 2.3 convolution_convert_fusion.1
  148.5 2.1 convolution_convert_fusion.refs_2_
  150.6 17.4 %exchange_7.1 = (bf16[4,64,1024]{2,1,0:T(8,128)(2,1)}, bf16[2,512,1024]{2,1,0:T(8,128)(2,1)}, bf16[2,1024,512]{2,1,0:T(8,128)(2,1)}) custom-call(bf16[4,64,1024]{2,1,0:T(8,128)(2,1)} %bitcast.180, bf16[2,512,1024]{2,1,0:T(8,128)(2,1)} %bitcast.154, bf16[1024,1024]{1,0:T(8,128)(2,1)} %convolution_convert_fusion.refs_2_), custom_call_target="tpu_custom_call" | custom-call | tf_op jit(solution)/shard_map/exchange_7/pallas_call | solution.py:142
  171.9 3.3 %reduce_sum.325.refs_1_ = bf16[512,1024]{1,0:T(8,128)(2,1)} reduce(bf16[2,512,1024]{2,1,0:T(8,128)(2,1)} %get-tuple-element.81, bf16[]{:T(256)} %constant.39.clone.1), dimensions={0}, to_apply=%region_8.9 | reduce | flops 524288 | bytes 3145730 | tf_op jit(solution)/shard_map/reduce_sum | solution.py:306
  175.3 17.5 %exchange_8.1 = (bf16[4,64,1024]{2,1,0:T(8,128)(2,1)}, bf16[4,512,256]{2,1,0:T(8,128)(2,1)}) custom-call(bf16[64,1024]{1,0:T(8,128)(2,1)} %add_convert_fusion.1.refs_0_, bf16[512,1024]{1,0:T(8,128)(2,1)} %reduce_sum.325.refs_1_), custom_call_target="tpu_custom_call" | custom-call | tf_op jit(solution)/shard_map/exchange_8/pallas_call | solution.py:142
  194.1 2.1 convolution_convert_fusion.3
  197.1 10.9 %exchange_9.1 = (bf16[4,256,64]{2,1,0:T(8,128)(2,1)}, bf16[4,32,1024]{2,1,0:T(8,128)(2,1)}, bf16[2,128,1024]{2,1,0:T(8,128)(2,1)}) custom-call(bf16[4,256,64]{2,1,0:T(8,128)(2,1)} %bitcast.172, bf16[4,32,1024]{2,1,0:T(8,128)(2,1)} %get-tuple-element.165.refs_1_, bf16[2,128,1024]{2,1,0:T(8,128)(2,1)} %bitcast.158), custom_call_target="tpu_custom_call" | custom-call | tf_op jit(solution)/shard_map/exchange_9/pallas_call | solution.py:142
  209.1 5.3 %attend_backward.1 = (f32[1024,64]{1,0:T(8,128)}, f32[1024,64]{1,0:T(8,128)}, f32[1024,64]{1,0:T(8,128)}) custom-call(bf16[1024,64]{1,0:T(8,128)(2,1)} %bitcast.152, bf16[1024,64]{1,0:T(8,128)(2,1)} %bitcast.150, bf16[1024,64]{1,0:T(8,128)(2,1)} %bitcast.148, bf16[1024,64]{1,0:T(8,128)(2,1)} %get-tuple-element.70.a_ref, ...), custom_call_target="tpu_custom_call" | custom-call | tf_op jit(solution)/shard_map/attend_backward/pallas_call | solution.py:224
  214.3 1.9 fusion.14
  219.7 17.6 %exchange_10.1 = (bf16[4,3,256,64]{3,2,1,0:T(8,128)(2,1)}, bf16[4,32,1024]{2,1,0:T(8,128)(2,1)}, bf16[4,128,256]{2,1,0:T(8,128)(2,1)}) custom-call(bf16[4,3,256,64]{3,2,1,0:T(8,128)(2,1)} %maximum_bitcast_fusion.refs_0_, bf16[4,32,1024]{2,1,0:T(8,128)(2,1)} %get-tuple-element.164.refs_1_, bf16[128,1024]{1,0:T(8,128)(2,1)} %reduce_sum.327.refs_2_), custom_call_target="tpu_custom_call" | custom-call | tf_op jit(solution)/shard_map/exchange_10/pallas_call | solution.py:142
  239.7 2.8 convolution_convert_fusion.7
  244.7 2.2 convert_reduce_fusion.1.refs_5_
  246.9 1.8 convolution_convert_fusion.2.refs_2_
  248.7 3.2 %reduce_sum.329 = bf16[1024,512]{1,0:T(8,128)(2,1)} reduce(bf16[2,1024,512]{2,1,0:T(8,128)(2,1)} %get-tuple-element.92, bf16[]{:T(256)} %constant.39.clone.1), dimensions={0}, to_apply=%region_12.13 | reduce | flops 524288 | bytes 3145730 | tf_op jit(solution)/shard_map/reduce_sum | solution.py:292
  252.0 17.2 %exchange_11.1 = (bf16[4,64,1024]{2,1,0:T(8,128)(2,1)}, bf16[4,256,512]{2,1,0:T(8,128)(2,1)}, bf16[2,1024,384]{2,1,0:T(8,128)(2,1)}) custom-call(bf16[4,64,1024]{2,1,0:T(8,128)(2,1)} %bitcast.157, bf16[4,256,512]{2,1,0:T(8,128)(2,1)} %bitcast.141, bf16[1024,768]{1,0:T(8,128)(2,1)} %convolution_convert_fusion.2.refs_2_), custom_call_target="tpu_custom_call" | custom-call | tf_op jit(solution)/shard_map/exchange_11/pallas_call | solution.py:142
  273.0 2.2 convert_reduce_fusion.refs_6_
  276.6 24.6 %exchange_12.1 = (bf16[16,64,64]{2,1,0:T(8,128)(2,1)}, bf16[16,64,64]{2,1,0:T(8,128)(2,1)}, f32[16,6,64]{2,1,0:T(8,128)}, f32[4,1,256]{2,1,0:T(1,128)}, bf16[4,2...) custom-call(bf16[16,64,64]{2,1,0:T(8,128)(2,1)} %get-tuple-element.163.refs_0_, ...), custom_call_target="tpu_custom_call" | custom-call | tf_op jit(solution)/shard_map/exchange_12/pallas_call | solution.py:142
  301.2 1.8 copy.55
  305.2 2.0 convert_reduce_fusion.2.refs_0_
  307.2 3.7 %exchange_13.1 = (f32[256,768]{1,0:T(8,128)}, f32[2,6,128]{2,1,0:T(8,128)}) custom-call(f32[256,384]{1,0:T(8,128)} %convert_reduce_fusion.2.refs_0_, f32[6,128]{1,0:T(8,128)} %maximum_bitcast_fusion.2.refs_1_), custom_call_target="tpu_custom_call" | custom-call | tf_op jit(solution)/shard_map/exchange_13/pallas_call | solution.py:142
  (180 shorter events, 57.3 us)
Async XLA Ops:
  35.5 7.3 %copy-start = (bf16[16,64,64]{2,1,0:T(8,128)(2,1)S(1)}, bf16[16,64,64]{2,1,0:T(8,128)(2,1)}, u32[]{:S(2)}) copy-start(bf16[16,64,64]{2,1,0:T(8,128)(2,1)} %get-tuple-element.61) | copy-start | bytes 393220
  35.5 7.3 %copy-start.1 = (bf16[16,64,64]{2,1,0:T(8,128)(2,1)S(1)}, bf16[16,64,64]{2,1,0:T(8,128)(2,1)}, u32[]{:S(2)}) copy-start(bf16[16,64,64]{2,1,0:T(8,128)(2,1)} %get-tuple-element.68) | copy-start | bytes 393220
  38.8 4.7 %copy-start.25 = (f32[64]{0:T(128)}, f32[64]{0:T(128)S(1)}, u32[]{:S(2)}) copy-start(f32[64]{0:T(128)S(1)} %get-tuple-element.183) | copy-start | bytes 772
  38.8 4.7 %copy-start.27 = (f32[64]{0:T(128)}, f32[64]{0:T(128)S(1)}, u32[]{:S(2)}) copy-start(f32[64]{0:T(128)S(1)} %get-tuple-element.184) | copy-start | bytes 772
  40.0 3.4 %copy-start.16 = (f32[1024]{0:T(1024)}, f32[1024]{0:T(1024)S(1)}, u32[]{:S(2)}) copy-start(f32[1024]{0:T(1024)S(1)} %mul.210) | copy-start | bytes 12292
  85.0 16.7 %copy-start.15 = (bf16[4,32,1024]{2,1,0:T(8,128)(2,1)S(1)}, bf16[4,32,1024]{2,1,0:T(8,128)(2,1)}, u32[]{:S(2)}) copy-start(bf16[4,32,1024]{2,1,0:T(8,128)(2,1)} %get-tuple-element.74) | copy-start | bytes 786436
  85.0 18.5 %copy-start.2 = (bf16[2,128,1024]{2,1,0:T(8,128)(2,1)S(1)}, bf16[2,128,1024]{2,1,0:T(8,128)(2,1)}, u32[]{:S(2)}) copy-start(bf16[2,128,1024]{2,1,0:T(8,128)(2,1)} %get-tuple-element.72) | copy-start | bytes 1572868
  121.8 49.3 %copy-start.21 = (f32[64]{0:T(128)}, f32[64]{0:T(128)S(1)}, u32[]{:S(2)}) copy-start(f32[64]{0:T(128)S(1)} %get-tuple-element.181) | copy-start | bytes 772
  121.8 49.3 %copy-start.23 = (f32[64]{0:T(128)}, f32[64]{0:T(128)S(1)}, u32[]{:S(2)}) copy-start(f32[64]{0:T(128)S(1)} %get-tuple-element.182) | copy-start | bytes 772
  138.4 2.6 copy-start.35
  146.3 2.3 copy-start.11
  169.4 5.8 %copy-start.29 = (f32[64]{0:T(128)}, f32[64]{0:T(128)S(1)}, u32[]{:S(2)}) copy-start(f32[64]{0:T(128)S(1)} %broadcast_multiply_fusion.3) | copy-start | bytes 772
  171.1 4.1 %copy-start.31 = (f32[64]{0:T(128)}, f32[64]{0:T(128)S(1)}, u32[]{:S(2)}) copy-start(f32[64]{0:T(128)S(1)} %broadcast_multiply_fusion.2) | copy-start | bytes 772
  209.1 8.5 %copy-start.9 = (bf16[2,128,1024]{2,1,0:T(8,128)(2,1)S(1)}, bf16[2,128,1024]{2,1,0:T(8,128)(2,1)}, u32[]{:S(2)}) copy-start(bf16[2,128,1024]{2,1,0:T(8,128)(2,1)} %get-tuple-element.89) | copy-start | bytes 1572868
  214.3 4.1 %copy-start.10 = (f32[1024,64]{1,0:T(8,128)S(1)}, f32[1024,64]{1,0:T(8,128)}, u32[]{:S(2)}) copy-start(f32[1024,64]{1,0:T(8,128)} %get-tuple-element.88) | copy-start | bytes 786436
  238.3 4.5 %copy-start.19 = (f32[1,16,64]{2,0,1:T(1,128)S(1)}, f32[1,16,64]{2,0,1:T(1,128)}, u32[]{:S(2)}) copy-start(f32[1,16,64]{2,0,1:T(1,128)} %get-tuple-element.170) | copy-start | bytes 12292
  238.3 4.5 %copy-start.22 = (f32[64]{0:T(128)S(1)}, f32[64]{0:T(128)}, u32[]{:S(2)}) copy-start(f32[64]{0:T(128)} %copy-done.21) | copy-start | bytes 772
  238.3 4.5 %copy-start.24 = (f32[64]{0:T(128)S(1)}, f32[64]{0:T(128)}, u32[]{:S(2)}) copy-start(f32[64]{0:T(128)} %copy-done.23) | copy-start | bytes 772
  238.3 4.5 %copy-start.30 = (f32[64]{0:T(128)S(1)}, f32[64]{0:T(128)}, u32[]{:S(2)}) copy-start(f32[64]{0:T(128)} %copy-done.29) | copy-start | bytes 772
  238.3 4.5 %copy-start.32 = (f32[64]{0:T(128)S(1)}, f32[64]{0:T(128)}, u32[]{:S(2)}) copy-start(f32[64]{0:T(128)} %copy-done.31) | copy-start | bytes 772
  242.8 4.1 %copy-start.7 = (bf16[4,64,1024]{2,1,0:T(8,128)(2,1)S(1)}, bf16[4,64,1024]{2,1,0:T(8,128)(2,1)}, u32[]{:S(2)}) copy-start(bf16[4,64,1024]{2,1,0:T(8,128)(2,1)} %get-tuple-element.64) | copy-start | bytes 1572868
  252.0 18.4 %copy-start.17 = (f32[1024]{0:T(1024)S(1)}, f32[1024]{0:T(1024)}, u32[]{:S(2)}) copy-start(f32[1024]{0:T(1024)} %copy-done.16) | copy-start | bytes 12292
  252.0 18.8 %copy-start.26 = (f32[64]{0:T(128)S(1)}, f32[64]{0:T(128)}, u32[]{:S(2)}) copy-start(f32[64]{0:T(128)} %copy-done.25) | copy-start | bytes 772
  252.0 18.8 %copy-start.28 = (f32[64]{0:T(128)S(1)}, f32[64]{0:T(128)}, u32[]{:S(2)}) copy-start(f32[64]{0:T(128)} %copy-done.27) | copy-start | bytes 772
  269.2 3.2 copy-start.18
  269.2 3.1 copy-start.20
  270.8 4.4 %copy-start.3 = (bf16[2,1024,384]{2,1,0:T(8,128)(2,1)S(1)}, bf16[2,1024,384]{2,1,0:T(8,128)(2,1)}, u32[]{:S(2)}) copy-start(bf16[2,1024,384]{2,1,0:T(8,128)(2,1)} %get-tuple-element.94) | copy-start | bytes 4718596
  301.2 12.4 %copy-start.12 = (bf16[16,64,64]{2,1,0:T(8,128)(2,1)S(1)}, bf16[16,64,64]{2,1,0:T(8,128)(2,1)}, u32[]{:S(2)}) copy-start(bf16[16,64,64]{2,1,0:T(8,128)(2,1)} %get-tuple-element.99) | copy-start | bytes 393220
  310.9 3.6 %copy-start.6 = (f32[256,768]{1,0:T(8,128)S(1)}, f32[256,768]{1,0:T(8,128)}, u32[]{:S(2)}) copy-start(f32[256,768]{1,0:T(8,128)} %get-tuple-element.104) | copy-start | bytes 2359300
  313.6 2.3 copy-start.14
  313.6 3.0 copy-start.5
  314.8 2.8 copy-start.4
  (4 other events, 6.5 us)
